TPU v7x, 768 devices: a whole 4x8x12 slice. The times are simulated.
768 devices in a mesh: gx: 48 (over z, x_hi, core), gy: 16 (over y, x_lo).
Axes of the slice: x: 4 (x_hi: 2, x_lo: 2; x = x_hi * 2 + x_lo), y: 8, z: 12, core: 2. Of those that a mesh axis runs over, the one named last changes fastest.
Arguments:
- e_field: float32 [3, 384, 128, 128], P(None, 'gx', 'gy'), may hold values from -6 to 6
- h_field: float32 [3, 384, 128, 128], P(None, 'gx', 'gy'), may hold values from -6 to 6
- current: float32 [3, 384, 128, 128], P(None, 'gx', 'gy'), may hold values from -4 to 4
- material: int32 [384, 128, 128], P('gx', 'gy'), may hold values from 0 to 7
- pole: int32 [384, 128, 128], P('gx', 'gy'), may hold values from 0 to 3
- permittivity: float32 [8], replicated, may hold values from 1 to 6
- conductivity: float32 [8], replicated, may hold values from 0.05 to 1
- plasma: float32 [4], replicated, may hold values from 0.1 to 2
- damping: float32 [4], replicated, may hold values from 0.05 to 1
- box: int32 [4], replicated, may hold values from 1 to 383, as said below
- spectral_slot: int32 [128], replicated, may hold values from 0 to 511
- ux_index: int32 [48], replicated, may hold values from 0 to 255
- uz_index: int32 [16], replicated, may hold values from 0 to 255
Outputs:
- e_final: float32 [3, 384, 128, 128], P(None, 'gx', 'gy')
- h_final: float32 [3, 384, 128, 128], P(None, 'gx', 'gy')
- current_final: float32 [3, 384, 128, 128], P(None, 'gx', 'gy')
- far_field: float32 [4, 48, 16, 128], P(None, 'gx', 'gy')
Inputs may be any that keep to these rules, and one draw needn't show every extreme that they name: box[0] = 1, box[1] = 383, 1 <= box[2] <= 32 and 96 <= box[3] <= 127.
All inputs are finite; a program needn't handle non-finite values.
Results may differ from a plain program's by a relative error of at most 0.0003.
Values sent between devices are 32-bit elements; how exact they have to be, the bound alone decides.
A program may use at most 32 MiB of HBM per device.

v0:
```python
import math

import jax
import jax.numpy as jnp
from jax import lax
from jax.sharding import PartitionSpec as P

MARCH_TOTAL = 3
SPECTRUM_POINTS = 512
AGRID = 256


delta_interval = 0.5
highest = lax.Precision.HIGHEST


def shifted(value, axis, steps):
    count = lax.axis_size(axis)
    initial, last = (max(0, -steps), min(count, count - steps))
    return lax.ppermute(value, axis, [(source, source + steps) for source in range(initial, last)])


def from_x(piece, offset):
    return shifted(piece, "gx", offset)


def from_y(piece, offset):
    return shifted(piece, "gy", offset)


def lookup(table, labels):
    total = jnp.zeros(labels.shape, jnp.float32)
    for entry in range(table.shape[0]):
        total = total + jnp.where(labels == entry, table[entry], 0.0)
    return total


def curl_of_h(h_field):
    lower_x = from_x(h_field[1:3, -1:], 1)
    lower_y = from_y(h_field[0::2, :, -1:], 1)
    prev_x = jnp.concatenate([lower_x, h_field[1:3, :-1]], axis=1)
    prev_y = jnp.concatenate([lower_y, h_field[0::2, :, :-1]], axis=2)
    prev_z = jnp.pad(h_field[0:2, :, :, :-1], ((0, 0), (0, 0), (0, 0), (1, 0)))
    first = h_field[2] - prev_y[1] - (h_field[1] - prev_z[1])
    second = h_field[0] - prev_z[0] - (h_field[2] - prev_x[1])
    third = h_field[1] - prev_x[0] - (h_field[0] - prev_y[0])
    return jnp.stack([first, second, third])


def curl_of_e(e_field):
    upper_x = from_x(e_field[1:3, :1], -1)
    upper_y = from_y(e_field[0::2, :, :1], -1)
    next_x = jnp.concatenate([e_field[1:3, 1:], upper_x], axis=1)
    next_y = jnp.concatenate([e_field[0::2, :, 1:], upper_y], axis=2)
    next_z = jnp.pad(e_field[0:2, :, :, 1:], ((0, 0), (0, 0), (0, 0), (0, 1)))
    first = next_y[1] - e_field[2] - (next_z[1] - e_field[1])
    second = next_z[0] - e_field[0] - (next_x[1] - e_field[2])
    third = next_x[0] - e_field[1] - (next_y[0] - e_field[0])
    return jnp.stack([first, second, third])


def rotation_table(angle):
    cosine, sine = (jnp.cos(angle), jnp.sin(angle))
    return jnp.stack([jnp.stack([cosine, sine]), jnp.stack([-sine, cosine])])


def body(
    e_field,
    h_field,
    current,
    material,
    pole,
    permittivity,
    conductivity,
    plasma,
    damping,
    box,
    spectral_slot,
    ux_index,
    uz_index,
):
    cells_x = e_field.shape[1]
    cells_y = e_field.shape[2]
    depth = e_field.shape[3]
    grid_x = cells_x * lax.axis_size("gx")
    grid_y = cells_y * lax.axis_size("gy")
    anchor_x = lax.axis_index("gx") * cells_x
    base_ordinate = lax.axis_index("gy") * cells_y
    dielectric_voxel = lookup(permittivity, material)
    sig_cell = lookup(conductivity, material)
    plasma_cell = lookup(plasma, pole)
    rate_cell = lookup(damping, pole)
    loss_term = sig_cell * delta_interval / (2.0 * dielectric_voxel)
    keep_e = (1.0 - loss_term) / (1.0 + loss_term)
    drive_e = delta_interval / dielectric_voxel / (1.0 + loss_term)
    half_rate = rate_cell * delta_interval / 2.0
    keep_j = (1.0 - half_rate) / (1.0 + half_rate)
    drive_j = plasma_cell * delta_interval / (1.0 + half_rate)
    x_cells = anchor_x + jnp.arange(cells_x)
    inside_x = ((x_cells >= box[0]) & (x_cells < box[1])).astype(jnp.float32)
    lower_row = box[2] - base_ordinate
    upper_row = box[3] - base_ordinate
    lower_in = (lower_row >= 0) & (lower_row < cells_y)
    upper_in = (upper_row >= 0) & (upper_row < cells_y)
    face_row = jnp.clip(jnp.where(upper_in, upper_row, lower_row), 0, cells_y - 1)
    face_sign = jnp.where(upper_in, 1.0, -1.0).astype(jnp.float32)
    face_cell = jnp.where(upper_in, box[3], box[2])
    weight = inside_x * (lower_in | upper_in).astype(jnp.float32)
    records = []
    for step_index in range(MARCH_TOTAL):
        current = keep_j * current + drive_j * e_field
        e_field = keep_e * e_field + drive_e * (curl_of_h(h_field) - current)
        h_field = h_field - delta_interval * curl_of_e(e_field)
        e_row = lax.dynamic_index_in_dim(e_field, face_row, axis=2, keepdims=False)
        h_row = lax.dynamic_index_in_dim(h_field, face_row, axis=2, keepdims=False)
        quantity = jnp.stack([h_row[2], -h_row[0], -e_row[2], e_row[0]])
        records.append(face_sign * quantity * weight[None, :, None])
    stacked = jnp.stack(records)
    drive_pulsation = math.pi * (spectral_slot.astype(jnp.float32) + 0.5) / SPECTRUM_POINTS
    heading_first = -0.7 + 1.4 * (ux_index.astype(jnp.float32) + 0.5) / AGRID
    heading_third = -0.7 + 1.4 * (uz_index.astype(jnp.float32) + 0.5) / AGRID
    heading_second = jnp.sqrt(1.0 - heading_first[:, None] ** 2 - heading_third[None, :] ** 2)
    tick_epochs = jnp.arange(1, MARCH_TOTAL + 1).astype(jnp.float32) * delta_interval
    cycle_exponent = drive_pulsation[:, None] * tick_epochs[None, :]
    time_table = jnp.stack([jnp.cos(cycle_exponent), -jnp.sin(cycle_exponent)])
    transformed = jnp.einsum("sfn,ncxz->sfcxz", time_table, stacked, precision=highest)
    third_location = (jnp.arange(depth) - depth // 2).astype(jnp.float32)
    third_bearing = (drive_pulsation[:, None] * heading_third[None, :])[
        :, None, :
    ] * third_location[None, :, None]
    along_z = jnp.einsum(
        "sfcxz,srfzj->rfcxj", transformed, rotation_table(third_bearing), precision=highest
    )
    first_location = (x_cells - grid_x // 2).astype(jnp.float32)
    first_bearing = (drive_pulsation[:, None] * heading_first[None, :])[
        :, None, :
    ] * first_location[None, :, None]
    x_direction_cells = jnp.einsum(
        "sfcxj,srfxi->rcijf", along_z, rotation_table(first_bearing), precision=highest
    )
    second_location = (face_cell - grid_y // 2).astype(jnp.float32)
    second_bearing = heading_second[:, :, None] * drive_pulsation[None, None, :] * second_location
    cos_y, sin_y = (jnp.cos(second_bearing), jnp.sin(second_bearing))
    refractive_real = x_direction_cells[0] * cos_y - x_direction_cells[1] * sin_y
    n_imag = x_direction_cells[0] * sin_y + x_direction_cells[1] * cos_y
    sine_theta = jnp.sqrt(1.0 - heading_third**2)
    ratio_a = (heading_first[:, None] * heading_third[None, :] / sine_theta[None, :])[:, :, None]
    ratio_b = (heading_second / sine_theta[None, :])[:, :, None]
    sine = sine_theta[None, :, None]
    divisor = math.sqrt(grid_x * depth)
    parts = []
    for block in (refractive_real, n_imag):
        parts.append((block[2] * ratio_b - block[0] * ratio_a + block[1] * sine) / divisor)
        parts.append((block[2] * ratio_a - block[3] * sine + block[0] * ratio_b) / divisor)
    partial_value = jnp.stack([parts[0], parts[2], parts[1], parts[3]])
    count_i = partial_value.shape[1]
    count_j = partial_value.shape[2]
    freqs = partial_value.shape[3]
    own_i = count_i // lax.axis_size("gx")
    own_j = count_j // lax.axis_size("gy")
    flattened = partial_value.reshape(4, count_i * count_j, freqs)
    owned = lax.psum_scatter(flattened, ("gx", "gy"), scatter_dimension=1, tiled=True)
    far_field = owned.reshape(4, own_i, own_j, freqs)
    return (e_field, h_field, current, far_field)


def solution(mesh):
    return jax.shard_map(
        body,
        mesh=mesh,
        in_specs=(
            P(None, "gx", "gy", None),
            P(None, "gx", "gy", None),
            P(None, "gx", "gy", None),
            P("gx", "gy", None),
            P("gx", "gy", None),
            P(),
            P(),
            P(),
            P(),
            P(),
            P(),
            P(),
            P(),
        ),
        out_specs=(
            P(None, "gx", "gy", None),
            P(None, "gx", "gy", None),
            P(None, "gx", "gy", None),
            P(None, "gx", "gy", None),
        ),
        check_vma=False,
    )
```

profile of v0, /device:TPU:1, one launch (start us, length us, event | category | flops | bytes accessed | tf_op | source)
XLA Modules:
  0.0 671.9 jit_solution(8051731170395281056)
XLA Ops:
  7.2 1.3 slice.465
  8.5 6.0 collective-permute-start.1
  14.5 0.9 copy.129
  16.0 2.8 collective-permute-start
  18.8 1.4 fusion.112
  21.6 1.4 fusion.116
  23.0 1.4 fusion.115
  24.4 1.6 fusion.114
  26.1 1.6 fusion.113
  31.3 0.8 multiply_sine_fusion.1
  32.1 0.9 maximum_bitcast_fusion.3
  33.7 3.7 multiply_sine_fusion
  37.5 4.8 fusion.19
  42.3 2.4 maximum_bitcast_fusion.1
  44.7 2.7 subtract_divide_fusion
  47.3 5.1 multiply_divide_fusion
  52.5 10.3 %subtract_divide_fusion.1 = (f32[8,8,128]{2,1,0:T(8,128)S(1)}, pred[8,8,128]{2,1,0:T(8,128)(4,1)S(1)}, pred[8,8,128]{2,1,0:T(8,128)(4,1)S(1)}, pred[8,8,128]{2,1...) fusion(f32[]{:T(128)} %bitcast.15, f32[]{:T(128)} %bitcast.14, ...), kind=kLoop, calls=%fused_computation.182 | loop fusion | flops 360448 | bytes 131136 | tf_op jit(solution)/shard_map/div | solution.py:94
  62.7 10.3 %multiply_divide_fusion.1 = f32[8,8,128]{2,1,0:T(8,128)S(1)} fusion(pred[8,8,128]{2,1,0:T(8,128)(4,1)S(1)} %get-tuple-element.30, f32[]{:T(128)} %bitcast.15, pred[8,8,128]{2,1,0:T(8,128)(4,1)S(1)} %get-tuple-element.29, pred[8,8,128]{2,1,0:T(8,128)(4,1)S(1)} %get-tuple-element.28, pred[8,8,128]{2,1,0:T(8,128)(4,1)S(1)} %get-tuple-element.27, ...), kind=kLoop, calls=%fused_computation.181 | loop fusion | flops 294912 | bytes 98368 | tf_op jit(solution)/shard_map/div | solution.py:95
  73.0 1.8 and_select_fusion
  79.1 3.0 copy.161
  82.2 0.9 fusion.37
  83.2 0.9 fusion.22
  84.0 7.3 %collective-permute-start.3 = (f32[2,1,8,128]{3,1,2,0:T(1,128)S(1)}, f32[2,1,8,128]{3,1,2,0:T(1,128)S(1)}, u32[]{:S(2)}, u32[]{:S(2)}) collective-permute-start(f32[2,1,8,128]{3,1,2,0:T(1,128)S(1)} %slice.590), channel_id=1, source_target_pairs={{16,0},{32,16},{48,32},{64,48},{80,64},{96,80},{112,96},{128,112},... | collective-permute-start | bytes 24584 | tf_op jit(solution)/shard_map/ppermute | solution.py:20
  91.3 1.3 collective-permute-start.2
  92.8 3.1 collective-permute-done.2
  96.0 1.9 collective-permute-start.5
  97.9 3.2 collective-permute-start.4
  102.0 0.9 fusion.25
  102.9 1.9 collective-permute-start.7
  104.9 1.3 collective-permute-start.6
  106.3 3.1 collective-permute-done.7
  109.6 6.6 collective-permute-start.9
  116.3 3.9 collective-permute-start.8
  121.1 0.7 fusion.28
  121.8 1.9 collective-permute-start.11
  123.7 1.8 collective-permute-start.10
  125.6 2.6 collective-permute-done.11
  128.6 3.5 convolution_bitcast_fusion
  132.1 17.9 %fusion.2 = f32[128,2,16,4,8,1]{2,4,5,1,3,0:T(8,128)S(1)} fusion(f32[2,128,4,8,128,1]{4,1,3,2,0,5:T(8,128)S(1)} %convolution_bitcast_fusion, f32[1,2,128,128,16]{3,4,2,1,0:T(8,128)S(1)} %copy-done.1, f32[1,2,128,128,16]{3,4,2,1,0:T(8,128)S(1)} %copy-done), kind=kOutput, calls=%fused_computation.5 | convolution fusion | flops 403701760 | bytes 8912896 | tf_op jit(solution)/shard_map/sfcxz,srfzj->rfcxj/dot_general | solution.py:131
  150.0 7.2 %fusion.5 = f32[2,4,48,16,128]{2,3,1,0,4:T(8,128)S(1)} fusion(f32[2,2,128,8,48,1]{4,3,0,5,1,2:T(8,128)S(1)} %copy.161, f32[128,2,16,4,8,1]{2,4,5,1,3,0:T(8,128)S(1)} %fusion.2), kind=kOutput, calls=%fused_computation.10 | convolution fusion | flops 150994944 | bytes 4456448 | tf_op jit(solution)/shard_map/sfcxj,srfxi->rcijf/dot_general | solution.py:138
  157.2 5.0 multiply_subtract_fusion
  162.2 4.1 fusion.17
  166.3 2.4 copy.151
  168.7 1.3 copy.150
  171.1 1.3 pad_maximum_fusion
  172.3 2.1 copy.152
  176.5 487.1 %all-reduce.9.cloned.1.call-done = f32[4,768,128]{2,0,1:T(4,128)} async-done(((f32[4,768,128]{2,0,1:T(4,128)}), f32[4,768,128]{2,0,1:T(4,128)}) %all-reduce.9.cloned.1.call-update) | async-done | bytes 1572880
  663.6 1.3 constant_dynamic-slice_fusion
  (109 shorter events, 13.7 us)
Async XLA Ops:
  7.2 656.4 %all-reduce.9.cloned.1.call-start = ((), (), s32[]{:S(2)}) async-start(), calls=%async_computation | async-start | bytes 3145728
  8.5 73.7 %collective-permute-start.1 = (f32[2,1,8,128]{3,1,2,0:T(1,128)}, f32[2,1,8,128]{3,1,2,0:T(1,128)}, u32[]{:S(2)}, u32[]{:S(2)}) collective-permute-start(f32[2,1,8,128]{3,1,2,0:T(1,128)} %bitcast.16), channel_id=1, source_target_pairs={{0,16},{16,32},{32,48},{48,64},{64,80},{80,96},{96,112},{112,128},... | collective-permute-start | bytes 24584 | tf_op jit(solution)/shard_map/ppermute | solution.py:20
  16.0 66.1 %collective-permute-start = (f32[2,8,1,128]{3,1,2,0:T(8,128)}, f32[2,8,1,128]{3,1,2,0:T(8,128)}, u32[]{:S(2)}, u32[]{:S(2)}) collective-permute-start(f32[2,8,1,128]{3,1,2,0:T(8,128)} %slice.457), channel_id=1, source_target_pairs={{0,1},{1,2},{2,3},{3,4},{4,5},{5,6},{6,7},{7,8},{8,9},{9,10},{10,1... | collective-permute-start | bytes 24584 | tf_op jit(solution)/shard_map/ppermute | solution.py:20
  31.2 11.0 %copy-start.13 = (f32[16]{0:T(128)}, f32[16]{0:T(128)S(1)}, u32[]{:S(2)}) copy-start(f32[16]{0:T(128)S(1)} %get-tuple-element.91) | copy-start | bytes 196
  42.3 2.4 copy-start.10
  42.3 10.2 %copy-start.11 = (s32[8,8,128]{2,1,0:T(8,128)S(1)}, s32[8,8,128]{2,1,0:T(8,128)}, u32[]{:S(2)}) copy-start(s32[8,8,128]{2,1,0:T(8,128)} %param.16) | copy-start | bytes 98308
  42.3 40.9 %copy-start.3 = (f32[3,8,8,128]{3,2,1,0:T(8,128)S(1)}, f32[3,8,8,128]{3,2,1,0:T(8,128)}, u32[]{:S(2)}) copy-start(f32[3,8,8,128]{3,2,1,0:T(8,128)} %param.13) | copy-start | bytes 294916
  42.3 40.9 %copy-start.4 = (f32[3,8,8,128]{3,2,1,0:T(8,128)S(1)}, f32[3,8,8,128]{3,2,1,0:T(8,128)}, u32[]{:S(2)}) copy-start(f32[3,8,8,128]{3,2,1,0:T(8,128)} %param.15) | copy-start | bytes 294916
  44.7 51.3 %copy-start.2 = (f32[3,8,8,128]{3,2,1,0:T(8,128)S(1)}, f32[3,8,8,128]{3,2,1,0:T(8,128)}, u32[]{:S(2)}) copy-start(f32[3,8,8,128]{3,2,1,0:T(8,128)} %param.14) | copy-start | bytes 294916
  82.1 39.0 %copy-start.5 = (f32[8,8,128]{2,0,1:T(8,128)S(1)}, f32[8,8,128]{2,0,1:T(8,128)}, u32[]{:S(2)}) copy-start(f32[8,8,128]{2,0,1:T(8,128)} %copy.139) | copy-start | bytes 98308
  82.1 39.0 %copy-start.6 = (f32[8,8,128]{2,0,1:T(8,128)S(1)}, f32[8,8,128]{2,0,1:T(8,128)}, u32[]{:S(2)}) copy-start(f32[8,8,128]{2,0,1:T(8,128)} %copy.137) | copy-start | bytes 98308
  82.1 39.0 %copy-start.7 = (f32[8,8,128]{2,0,1:T(8,128)S(1)}, f32[8,8,128]{2,0,1:T(8,128)}, u32[]{:S(2)}) copy-start(f32[8,8,128]{2,0,1:T(8,128)} %copy.128) | copy-start | bytes 98308
  82.1 39.0 %copy-start.8 = (f32[8,8,128]{2,0,1:T(8,128)S(1)}, f32[8,8,128]{2,0,1:T(8,128)}, u32[]{:S(2)}) copy-start(f32[8,8,128]{2,0,1:T(8,128)} %copy.126) | copy-start | bytes 98308
  82.2 46.4 %copy-start.15 = (f32[8]{0:T(128)S(1)}, f32[8]{0:T(128)}, u32[]{:S(2)}) copy-start(f32[8]{0:T(128)} %and_select_fusion) | copy-start | bytes 100
  82.2 46.4 %copy-start.12 = (f32[2,128,3,1,1]{1,0,2,4,3:T(2,128)S(1)}, f32[2,128,3,1,1]{1,0,2,4,3:T(2,128)}, u32[]{:S(2)}) copy-start(f32[2,128,3,1,1]{1,0,2,4,3:T(2,128)} %maximum_bitcast_fusion.6) | copy-start | bytes 9220
  84.0 8.7 %collective-permute-start.3 = (f32[2,1,8,128]{3,1,2,0:T(1,128)S(1)}, f32[2,1,8,128]{3,1,2,0:T(1,128)S(1)}, u32[]{:S(2)}, u32[]{:S(2)}) collective-permute-start(f32[2,1,8,128]{3,1,2,0:T(1,128)S(1)} %slice.590), channel_id=1, source_target_pairs={{16,0},{32,16},{48,32},{64,48},{80,64},{96,80},{112,96},{128,112},... | collective-permute-start | bytes 24584 | tf_op jit(solution)/shard_map/ppermute | solution.py:20
  91.3 4.5 collective-permute-start.2
  96.0 5.2 collective-permute-start.5
  97.9 4.0 collective-permute-start.4
  102.9 6.5 collective-permute-start.7
  104.9 4.7 collective-permute-start.6
  106.3 25.8 %copy-start = (f32[1,2,128,128,16]{3,4,2,1,0:T(8,128)S(1)}, f32[1,2,128,128,16]{3,4,2,1,0:T(8,128)}, u32[]{:S(2)}) copy-start(f32[1,2,128,128,16]{3,4,2,1,0:T(8,128)} %get-tuple-element.42) | copy-start | bytes 6291460
  106.3 25.8 %copy-start.1 = (f32[1,2,128,128,16]{3,4,2,1,0:T(8,128)S(1)}, f32[1,2,128,128,16]{3,4,2,1,0:T(8,128)}, u32[]{:S(2)}) copy-start(f32[1,2,128,128,16]{3,4,2,1,0:T(8,128)} %get-tuple-element.43) | copy-start | bytes 6291460
  109.6 10.6 %collective-permute-start.9 = (f32[2,1,8,128]{3,1,2,0:T(1,128)S(1)}, f32[2,1,8,128]{3,1,2,0:T(1,128)S(1)}, u32[]{:S(2)}, u32[]{:S(2)}) collective-permute-start(f32[2,1,8,128]{3,1,2,0:T(1,128)S(1)} %slice.619), channel_id=1, source_target_pairs={{0,16},{16,32},{32,48},{48,64},{64,80},{80,96},{96,112},{112,128},... | collective-permute-start | bytes 24584 | tf_op jit(solution)/shard_map/ppermute | solution.py:20
  116.3 4.7 collective-permute-start.8
  121.8 6.5 collective-permute-start.11
  123.7 4.7 collective-permute-start.10
  157.2 5.0 copy-start.14
  171.1 4.1 copy-start.9
Sparse Core Ops, SparseCore 0:
  174.6 488.9 all-reduce.8
where the time goes:
time: 681 us; the launch traced here: 672 us
  waiting for transfers between devices  498 us (73%)
  other arithmetic  59.9 us (9%)
  starting transfers between devices  40.1 us (6%)
  matrix products  28.6 us (4%)
  local copies, waits for them, and re-layouts  28.2 us (4%)
  between operations  17.6 us (3%)
    unnamed x2, waiting for transfers between devices  487 us
    ppermute x12, starting transfers between devices, shifted(): lax.ppermute(value, axis, [(source, source + steps) for source in range(i...  40 us
    dot_general x1, matrix products, body(): jnp.einsum('sfcxz,srfzj->rfcxj', transformed, rotation_table(third_bearin...  17.9 us
  transfers between devices with their start and end apart: 13, of which 8 were waited for; matrix products, arithmetic and copies ran while one was open for 10% of the time, Pallas kernels for 0%

commit v1 on v0

v1 whole, which is shorter than its diff:
```python
import math

import jax
import jax.numpy as jnp
from jax import lax
from jax.experimental import pallas as pl
from jax.experimental.pallas import tpu as pltpu
from jax.sharding import PartitionSpec as P

STEPS = 3
SPECTRUM_POINTS = 512
AGRID = 256
DT = 0.5
MESH = pl.DeviceIdType.MESH
F32 = jnp.float32
HIGHEST = lax.Precision.HIGHEST
TWO_OVER_PI = 0.6366197723675814
HALF_PI_HIGH = 1.5703125
HALF_PI_LOW = 4.838267948966e-4


def sincos(angle):
    turns = jnp.round(angle * TWO_OVER_PI)
    rest = (angle - turns * HALF_PI_HIGH) - turns * HALF_PI_LOW
    square = rest * rest
    sine = rest + rest * square * (
        -1.6666654611e-1 + square * (8.3321608736e-3 + square * -1.9515295891e-4)
    )
    cosine = (
        1.0
        - 0.5 * square
        + square
        * square
        * (4.166664568298827e-2 + square * (-1.388731625493765e-3 + square * 2.443315711809948e-5))
    )
    quadrant = turns.astype(jnp.int32)
    odd = (quadrant & 1) != 0
    sine_part = jnp.where(odd, cosine, sine)
    cosine_part = jnp.where(odd, sine, cosine)
    sine_out = jnp.where((quadrant & 2) != 0, -sine_part, sine_part)
    cosine_out = jnp.where(((quadrant + 1) & 2) != 0, -cosine_part, cosine_part)
    return cosine_out, sine_out


def make_kernel(sizes):
    gx_count, gy_count, cx, cy, depth, freqs, dirs_x = sizes
    half = cx
    tiles = dirs_x // 8

    def kernel(
        e_in,
        h_in,
        j_in,
        m_in,
        p_in,
        permittivity,
        conductivity,
        plasma,
        damping,
        box,
        ux_index,
        uz_index,
        slot,
        e_out,
        h_out,
        j_out,
        far_out,
        E,
        H,
        J,
        M,
        Q,
        K,
        S,
        R,
        C,
        G,
        A,
        TZ,
        TX,
        TY,
        PART,
        RX,
        local_sem,
        halo_send,
        halo_recv,
        rs_send,
        rs_recv,
        ag_send,
        ag_recv,
        gx_send,
        gx_recv,
    ):
        gx = lax.axis_index("gx")
        gy = lax.axis_index("gy")
        left = lax.rem(gx + gx_count - 1, gx_count)
        right = lax.rem(gx + 1, gx_count)
        below = lax.rem(gy + gy_count - 1, gy_count)
        above = lax.rem(gy + 1, gy_count)
        side = lax.div(gy, half)
        member = lax.rem(gy, half)

        own = (slice(None), pl.ds(0, cx), pl.ds(0, cy))
        local = [
            pltpu.make_async_copy(e_in, E.at[:, 0:cx, 0:cy, :], local_sem.at[0]),
            pltpu.make_async_copy(h_in, H.at[0, :, 0:cx, 0:cy, :], local_sem.at[1]),
            pltpu.make_async_copy(j_in, J.at[:, 0:cx, 0:cy, :], local_sem.at[2]),
            pltpu.make_async_copy(m_in, M.at[0:cx, 0:cy, :], local_sem.at[3]),
            pltpu.make_async_copy(p_in, Q.at[0:cx, 0:cy, :], local_sem.at[4]),
        ]
        for copy in local:
            copy.start()

        barrier = pltpu.get_barrier_semaphore()
        for place in ((left, above), (right, below)):
            pl.semaphore_signal(barrier, inc=1, device_id=place, device_id_type=MESH)

        def greet_row(step, carry):
            place = (lax.rem(gx + step, gx_count), gy)
            pl.semaphore_signal(barrier, inc=1, device_id=place, device_id_type=MESH)
            return carry

        def greet_column(step, carry):
            place = (gx, lax.rem(gy + step, gy_count))
            pl.semaphore_signal(barrier, inc=1, device_id=place, device_id_type=MESH)
            return carry

        lax.fori_loop(1, gy_count, greet_column, 0)
        lax.fori_loop(1, gx_count, greet_row, 0)

        omega = math.pi * (slot[...].astype(F32) + 0.5) / SPECTRUM_POINTS
        uz_own = -0.7 + 1.4 * (jnp.full((1, freqs), uz_index[gy], jnp.int32).astype(F32) + 0.5) / AGRID
        place_z = (lax.broadcasted_iota(jnp.int32, (depth, freqs), 0) - depth // 2).astype(F32)
        cos_z, sin_z = sincos((omega * uz_own) * place_z)
        TZ[:, 0:freqs] = cos_z
        TZ[:, freqs:] = sin_z

        sublane = lax.broadcasted_iota(jnp.int32, (8, freqs), 0)
        ux_tiles = []
        for tile in range(tiles):
            labels = jnp.zeros((8, freqs), jnp.int32)
            for row in range(8):
                labels = jnp.where(sublane == row, ux_index[tile * 8 + row], labels)
            ux_tiles.append(labels)
        ux = -0.7 + 1.4 * (jnp.concatenate(ux_tiles, axis=0).astype(F32) + 0.5) / AGRID
        omega_ux = omega * ux

        def fill_x(cell, carry):
            place_x = jnp.full((1, 1), gx * cx + cell - (gx_count * cx) // 2, jnp.int32).astype(F32)
            cos_x, sin_x = sincos(omega_ux * place_x)
            TX[0, cell] = cos_x
            TX[1, cell] = sin_x
            return carry

        lax.fori_loop(0, cx, fill_x, 0)
        uy = jnp.sqrt(1.0 - ux**2 - uz_own**2)
        for face in range(2):
            place_y = jnp.full((1, 1), box[2 + face] - (gy_count * cy) // 2, jnp.int32).astype(F32)
            cos_y, sin_y = sincos((omega * uy) * place_y)
            TY[face, 0] = cos_y
            TY[face, 1] = sin_y

        for copy in local:
            copy.wait()
        pl.semaphore_wait(barrier, gx_count - 1 + gy_count - 1 + 2)

        def halo(level):
            field = H.at[level]
            routes = [
                (field.at[:, 0, 0:cy, :], field.at[:, cx, 0:cy, :], (left, gy)),
                (field.at[:, cx - 1, 0:cy, :], field.at[:, cx + 1, 0:cy, :], (right, gy)),
                (field.at[:, 0:cx, 0, :], field.at[:, 0:cx, cy, :], (gx, below)),
                (field.at[:, 0:cx, cy - 1, :], field.at[:, 0:cx, 2 * cy - 1, :], (gx, above)),
                (field.at[0, 0, cy - 1, :], field.at[0, cx, 2 * cy - 1, :], (left, above)),
                (field.at[1, cx - 1, 0, :], field.at[1, cx + 1, cy, :], (right, below)),
            ]
            if level == 0:
                for ref in (E, J):
                    routes.append((ref.at[:, 0, 0:cy, :], ref.at[:, cx, 0:cy, :], (left, gy)))
                    routes.append((ref.at[:, 0:cx, 0, :], ref.at[:, 0:cx, cy, :], (gx, below)))
                for ref in (M, Q):
                    routes.append((ref.at[0, 0:cy, :], ref.at[cx, 0:cy, :], (left, gy)))
                    routes.append((ref.at[0:cx, 0, :], ref.at[0:cx, cy, :], (gx, below)))
            copies = []
            for index, (source, target, place) in enumerate(routes):
                copy = pltpu.make_async_remote_copy(
                    src_ref=source,
                    dst_ref=target,
                    send_sem=halo_send.at[level, index],
                    recv_sem=halo_recv.at[level, index],
                    device_id=place,
                    device_id_type=MESH,
                )
                copy.start()
                copies.append(copy)
            return copies

        pending = halo(0)

        planes, rows = cx + 1, 2 * cy
        row = lax.broadcasted_iota(jnp.int32, (1, rows, depth), 1)
        lane = lax.broadcasted_iota(jnp.int32, (1, 1, depth), 2)
        first_row = (row == 0) & (gy == 0)
        outer_row = (row >= cy) & (gy == gy_count - 1)

        def prev_y(value):
            return jnp.where(first_row, 0.0, pltpu.roll(value, 1, 1))

        def prev_z(value):
            return jnp.where(lane == 0, 0.0, pltpu.roll(value, 1, 2))

        def next_z(value):
            return jnp.where(lane == depth - 1, 0.0, pltpu.roll(value, depth - 1, 2))

        table_row = lax.broadcasted_iota(jnp.int32, (8, depth), 0)

        def table(source, count):
            values = jnp.ones((8, depth), F32)
            for entry in range(count):
                values = jnp.where(table_row == entry, source[entry], values)
            return values

        eps_table = table(permittivity, 8)
        sig_table = table(conductivity, 8)
        plasma_table = table(plasma, 4)
        damping_table = table(damping, 4)
        loss = sig_table * DT / (2.0 * eps_table)
        keep_e_table = (1.0 - loss) / (1.0 + loss)
        drive_e_table = DT / eps_table / (1.0 + loss)
        rate = damping_table * DT / 2.0
        keep_j_table = (1.0 - rate) / (1.0 + rate)
        drive_j_table = plasma_table * DT / (1.0 + rate)

        y_row = lax.broadcasted_iota(jnp.int32, (1, cy, depth), 1) + gy * cy
        face_weight = jnp.where(y_row == box[3], 1.0, 0.0) - jnp.where(y_row == box[2], 1.0, 0.0)
        x_cell = lax.broadcasted_iota(jnp.int32, (cx, depth), 0) + gx * cx
        inside = jnp.where((x_cell >= box[0]) & (x_cell < box[1]), 1.0, 0.0)

        def scatter(step):
            copies = []
            for offset in range(1, half):
                other = lax.rem(member + offset, half)
                copy = pltpu.make_async_remote_copy(
                    src_ref=S.at[step, :, pl.ds(other, 1), :],
                    dst_ref=R.at[step, :, pl.ds(member, 1), :],
                    send_sem=rs_send.at[step, offset],
                    recv_sem=rs_recv.at[step, offset],
                    device_id=(gx, side * half + other),
                    device_id_type=MESH,
                )
                copy.start()
                copies.append(copy)
            R[step, :, pl.ds(member, 1), :] = S[step, :, pl.ds(member, 1), :]
            return copies

        def gather(step):
            total = jnp.sum(R[step], axis=1, keepdims=True)
            C[step, :, 0:1, :] = total
            copies = []
            for offset in range(1, gy_count):
                other = lax.rem(gy + offset, gy_count)
                copy = pltpu.make_async_remote_copy(
                    src_ref=C.at[step, :, pl.ds(0, 1), :],
                    dst_ref=G.at[step, :, pl.ds(gy, 1), :],
                    send_sem=ag_send.at[step, offset],
                    recv_sem=ag_recv.at[step, offset],
                    device_id=(gx, other),
                    device_id_type=MESH,
                )
                copy.start()
                copies.append(copy)
            G[step, :, pl.ds(gy, 1), :] = total
            return copies

        scatters = []
        gathers = []
        halos = []
        for step in range(STEPS):
            for copy in pending:
                copy.wait_recv()
            if step == 0:
                for copy in pending[6:10]:
                    copy.wait_send()
                halos.extend(pending[:6] + pending[10:])
            else:
                halos.extend(pending)
            if step == 0:
                material = M[...]
                pole = Q[...]
                plane = lax.broadcasted_iota(jnp.int32, (planes, rows, depth), 0)
                outside = outer_row | ((plane == cx) & (gx == gx_count - 1))
                keep_e = jnp.zeros((planes, rows, depth), F32)
                drive_e = jnp.zeros((planes, rows, depth), F32)
                for entry in range(8):
                    hit = material == entry
                    keep_e = jnp.where(hit, keep_e_table[entry : entry + 1, :][None], keep_e)
                    drive_e = jnp.where(hit, drive_e_table[entry : entry + 1, :][None], drive_e)
                keep_j = jnp.zeros((planes, rows, depth), F32)
                drive_j = jnp.zeros((planes, rows, depth), F32)
                for entry in range(4):
                    hit = pole == entry
                    keep_j = jnp.where(hit, keep_j_table[entry : entry + 1, :][None], keep_j)
                    drive_j = jnp.where(hit, drive_j_table[entry : entry + 1, :][None], drive_j)
                K[0] = jnp.where(outside, 0.0, keep_e)
                K[1] = jnp.where(outside, 0.0, drive_e)
                K[2] = keep_j
                K[3] = drive_j
            hx = H[step, 0, 0:planes]
            hy = H[step, 1, 0:planes]
            hz = H[step, 2, 0:planes]
            edge_y = jnp.where(gx == 0, 0.0, H[step, 1, planes : planes + 1])
            edge_z = jnp.where(gx == 0, 0.0, H[step, 2, planes : planes + 1])
            hy_x = jnp.concatenate([edge_y, hy[0 : planes - 1]], axis=0)
            hz_x = jnp.concatenate([edge_z, hz[0 : planes - 1]], axis=0)
            curls = (
                hz - prev_y(hz) - (hy - prev_z(hy)),
                hx - prev_z(hx) - (hz - hz_x),
                hy - hy_x - (hx - prev_y(hx)),
            )
            fresh = []
            for axis in range(3):
                old = E[axis]
                flow = K[2] * J[axis] + K[3] * old
                J[axis] = flow
                value = K[0] * old + K[1] * (curls[axis] - flow)
                E[axis] = value
                fresh.append(value)
            ex, ey, ez = fresh
            ex_o, ey_o, ez_o = (value[0:cx, 0:cy] for value in fresh)
            ex_y = pltpu.roll(ex, rows - 1, 1)[0:cx, 0:cy]
            ez_y = pltpu.roll(ez, rows - 1, 1)[0:cx, 0:cy]
            ey_x = ey[1 : cx + 1, 0:cy]
            ez_x = ez[1 : cx + 1, 0:cy]
            first = ez_y - ez_o - (next_z(ey_o) - ey_o)
            second = next_z(ex_o) - ex_o - (ez_x - ez_o)
            third = ey_x - ey_o - (ex_y - ex_o)
            new_h = []
            for axis, turn in enumerate((first, second, third)):
                value = H[step, axis, 0:cx, 0:cy] - DT * turn
                H[step + 1, axis, 0:cx, 0:cy] = value
                new_h.append(value)
            if step + 1 < STEPS:
                pending = halo(step + 1)
            for index, value in enumerate((new_h[2], -new_h[0], -ez_o, ex_o)):
                S[step, index] = jnp.sum(value * face_weight, axis=1) * inside
            scatters.append(scatter(step))
            if step > 0:
                for copy in scatters[step - 1]:
                    copy.wait_recv()
                gathers.append(gather(step - 1))
        results = [
            pltpu.make_async_copy(E.at[:, 0:cx, 0:cy, :], e_out, local_sem.at[0]),
            pltpu.make_async_copy(H.at[STEPS, :, 0:cx, 0:cy, :], h_out, local_sem.at[1]),
            pltpu.make_async_copy(J.at[:, 0:cx, 0:cy, :], j_out, local_sem.at[2]),
        ]
        for copy in results:
            copy.start()
        for copy in scatters[STEPS - 1]:
            copy.wait_recv()
        gathers.append(gather(STEPS - 1))

        real = [jnp.zeros((8, freqs), F32) for _ in range(8)]
        imag = [jnp.zeros((8, freqs), F32) for _ in range(8)]
        for step in range(STEPS):
            for copy in gathers[step]:
                copy.wait_recv()
            lines = jnp.dot(
                G[step].reshape(4 * gy_count, depth),
                TZ[...],
                precision=HIGHEST,
                preferred_element_type=F32,
            )
            cos_t, sin_t = sincos(omega * ((step + 1) * DT))
            for index in range(8):
                along_cos = lines[index * 8 : index * 8 + 8, 0:freqs]
                along_sin = lines[index * 8 : index * 8 + 8, freqs:]
                real[index] = real[index] + (along_cos * cos_t + along_sin * sin_t)
                imag[index] = imag[index] + (along_sin * cos_t - along_cos * sin_t)
        for index in range(8):
            A[index, 0] = real[index]
            A[index, 1] = imag[index]

        sine_theta = jnp.sqrt(1.0 - uz_own**2)
        scale = 1.0 / math.sqrt(gx_count * cx * depth)
        uz_over = uz_own / sine_theta
        inverse = 1.0 / sine_theta

        def project(tile, carry):
            start = pl.multiple_of(tile * 8, 8)
            span = pl.ds(start, 8)
            sums = []
            for index in range(8):
                total_re = jnp.zeros((8, freqs), F32)
                total_im = jnp.zeros((8, freqs), F32)
                for cell in range(cx):
                    a_re = A[index, 0, cell : cell + 1, :]
                    a_im = A[index, 1, cell : cell + 1, :]
                    c = TX[0, cell, span, :]
                    s = TX[1, cell, span, :]
                    total_re = total_re + (a_re * c - a_im * s)
                    total_im = total_im + (a_re * s + a_im * c)
                sums.append((total_re, total_im))
            turned = []
            for comp in range(4):
                out_re = jnp.zeros((8, freqs), F32)
                out_im = jnp.zeros((8, freqs), F32)
                for face in range(2):
                    value_re, value_im = sums[comp * 2 + face]
                    c = TY[face, 0, span, :]
                    s = TY[face, 1, span, :]
                    out_re = out_re + (value_re * c - value_im * s)
                    out_im = out_im + (value_re * s + value_im * c)
                turned.append((out_re * scale, out_im * scale))
            ux_here = TX[2, 0, span, :]
            uy_here = TX[2, 1, span, :]
            ratio_a = ux_here * uz_over
            ratio_b = uy_here * inverse
            for part in range(2):
                nx, nz, lx, lz = (turned[comp][part] for comp in range(4))
                PART[part, span, :] = lx * ratio_b - nx * ratio_a + nz * sine_theta
                PART[2 + part, span, :] = lx * ratio_a - lz * sine_theta + nx * ratio_b
            return carry

        TX[2, 0] = ux + jnp.zeros((dirs_x, freqs), F32)
        TX[2, 1] = uy
        lax.fori_loop(0, tiles, project, 0)

        def exchange(step):
            other = lax.rem(gx + step, gx_count)
            return pltpu.make_async_remote_copy(
                src_ref=PART.at[:, pl.ds(other, 1), :],
                dst_ref=RX.at[:, pl.ds(gx, 1), :],
                send_sem=gx_send.at[step],
                recv_sem=gx_recv.at[step],
                device_id=(other, gy),
                device_id_type=MESH,
            )

        def send(step, carry):
            exchange(step).start()
            return carry

        def receive(step, carry):
            exchange(step).wait_recv()
            return carry

        def finish(step, carry):
            exchange(step).wait_send()
            return carry

        lax.fori_loop(1, gx_count, send, 0)
        RX[:, pl.ds(gx, 1), :] = PART[:, pl.ds(gx, 1), :]
        for group in halos, *scatters, *gathers:
            for copy in group:
                copy.wait_send()
        for copy in results:
            copy.wait()
        lax.fori_loop(1, gx_count, receive, 0)
        far_out[...] = jnp.sum(RX[...], axis=1, keepdims=True)
        lax.fori_loop(1, gx_count, finish, 0)

    return kernel


def solution(mesh):
    gx_count = mesh.shape["gx"]
    gy_count = mesh.shape["gy"]

    def body(
        e_field,
        h_field,
        current,
        material,
        pole,
        permittivity,
        conductivity,
        plasma,
        damping,
        box,
        spectral_slot,
        ux_index,
        uz_index,
    ):
        _, cx, cy, depth = e_field.shape
        freqs = spectral_slot.shape[0]
        dirs_x = ux_index.shape[0]
        anywhere = pl.BlockSpec(memory_space=pl.ANY)
        scalars = pl.BlockSpec(memory_space=pltpu.SMEM)
        vectors = pl.BlockSpec(memory_space=pltpu.VMEM)
        field = jax.ShapeDtypeStruct(e_field.shape, F32)
        e_field, h_field, current, far = pl.pallas_call(
            make_kernel((gx_count, gy_count, cx, cy, depth, freqs, dirs_x)),
            out_shape=(field, field, field, jax.ShapeDtypeStruct((4, 1, freqs), F32)),
            in_specs=[anywhere] * 5 + [scalars] * 7 + [vectors],
            out_specs=(anywhere, anywhere, anywhere, vectors),
            scratch_shapes=[
                pltpu.VMEM((3, cx + 1, 2 * cy, depth), F32),
                pltpu.VMEM((STEPS + 1, 3, cx + 2, 2 * cy, depth), F32),
                pltpu.VMEM((3, cx + 1, 2 * cy, depth), F32),
                pltpu.VMEM((cx + 1, 2 * cy, depth), jnp.int32),
                pltpu.VMEM((cx + 1, 2 * cy, depth), jnp.int32),
                pltpu.VMEM((4, cx + 1, 2 * cy, depth), F32),
                pltpu.VMEM((STEPS, 4, cx, depth), F32),
                pltpu.VMEM((STEPS, 4, cx, depth), F32),
                pltpu.VMEM((STEPS, 4, 8, depth), F32),
                pltpu.VMEM((STEPS, 4, gy_count, depth), F32),
                pltpu.VMEM((8, 2, cx, freqs), F32),
                pltpu.VMEM((depth, 2 * freqs), F32),
                pltpu.VMEM((3, cx, dirs_x, freqs), F32),
                pltpu.VMEM((2, 2, dirs_x, freqs), F32),
                pltpu.VMEM((4, dirs_x, freqs), F32),
                pltpu.VMEM((4, gx_count, freqs), F32),
                pltpu.SemaphoreType.DMA((5,)),
                pltpu.SemaphoreType.DMA((STEPS, 14)),
                pltpu.SemaphoreType.DMA((STEPS, 14)),
                pltpu.SemaphoreType.DMA((STEPS, cx)),
                pltpu.SemaphoreType.DMA((STEPS, cx)),
                pltpu.SemaphoreType.DMA((STEPS, gy_count)),
                pltpu.SemaphoreType.DMA((STEPS, gy_count)),
                pltpu.SemaphoreType.DMA((gx_count,)),
                pltpu.SemaphoreType.DMA((gx_count,)),
            ],
            compiler_params=pltpu.CompilerParams(collective_id=0, has_side_effects=True),
        )(
            e_field,
            h_field,
            current,
            material,
            pole,
            permittivity,
            conductivity,
            plasma,
            damping,
            box,
            ux_index,
            uz_index,
            spectral_slot.reshape(1, freqs),
        )
        return e_field, h_field, current, far.reshape(4, 1, 1, freqs)

    fields = P(None, "gx", "gy", None)
    cells = P("gx", "gy", None)
    return jax.shard_map(
        body,
        mesh=mesh,
        in_specs=(fields, fields, fields, cells, cells) + (P(),) * 8,
        out_specs=(fields,) * 4,
        check_vma=False,
    )
```

time: 681 us -> 60.4 us (0.09); the launches traced: 672 us -> 60.2 us
  waiting for transfers between devices: 498 us -> 0 us
  other arithmetic: 59.9 us -> 0 us
  Pallas kernels: 0 us -> 55.8 us
  starting transfers between devices: 40.1 us -> 0 us
  matrix products: 28.6 us -> 0 us
  local copies, waits for them, and re-layouts: 28.2 us -> 3.74 us
  between operations: 17.6 us -> 0.66 us
    unnamed x2 -> x0, waiting for transfers between devices: 487 us -> none
    pallas_call x0 -> x1, Pallas kernels: none -> 55.8 us  [body(): pl.pallas_call(make_kernel((gx_count, gy_count, cx, cy, depth, freqs, dir...]
    ppermute x12 -> x0, starting transfers between devices: 40 us -> none  [shifted(): lax.ppermute(value, axis, [(source, source + steps) for source in range(i...]
    div x7 -> x0, other arithmetic: 33.1 us -> none  [the longest x1 10.3 us: body(): keep_e = (1.0 - loss_term) / (1.0 + loss_term)]
    dot_general x3 -> x0, matrix products: 28.6 us -> none  [the longest x1 17.9 us: body(): jnp.einsum('sfcxz,srfzj->rfcxj', transformed, rotation_table(third_bearin...]
    slice x35 -> x0, local copies, waits for them, and re-layouts: 11.7 us -> none  [the longest x4 6.08 us: lookup(): total = total + jnp.where(labels == entry, table[entry], 0.0)]
    ppermute x12 -> x0, waiting for transfers between devices: 10.5 us -> none  [shifted(): lax.ppermute(value, axis, [(source, source + steps) for source in range(i...]
    div x8 -> x0, local copies, waits for them, and re-layouts: 7.2 us -> none  [the longest x2 3.7 us: body(): (block[2] * ratio_a - block[3] * sine + block[0] * ratio_b) / divisor]
  transfers between devices with their start and end apart: 13 -> 0, of which waited for: 8 -> 0; matrix products, arithmetic and copies ran while one was open for 10% -> 0% of each run, Pallas kernels for 0% -> 0%
where the time goes in v1:
time: 60.4 us; the launch traced here: 60.2 us
  Pallas kernels  55.8 us (92%)
  local copies, waits for them, and re-layouts  3.74 us (6%)
  between operations  0.66 us (1%)
    pallas_call x1, Pallas kernels, body(): pl.pallas_call(make_kernel((gx_count, gy_count, cx, cy, depth, freqs, dir...  55.8 us
    unnamed x10, local copies, waits for them, and re-layouts  3.74 us

profile of v1, /device:TPU:1, one launch (start us, length us, event | category | flops | bytes accessed | tf_op | source)
XLA Modules:
  0.0 60.2 jit_solution(6219974504977178705)
XLA Ops:
  0.6 55.8 %shard_map.156 = (f32[3,8,8,128]{3,2,1,0:T(8,128)}, f32[3,8,8,128]{3,2,1,0:T(8,128)}, f32[3,8,8,128]{3,2,1,0:T(8,128)}, f32[4,1,128]{2,1,0:T(1,128)}) custom-call(f32[3,8,8,128]{3,2,1,0:T(8,128)} %e_in.1, f32[3,8,8,128]{3,2,1,0:T(8,128)} %h_in.1, f32[3,8,8,128]{3,2,1,0:T(8,128)} %j_in.1, s32[8,8,128]{2,1,0:T(8,128)} %m_in.1, s32[8,8,128]{2,1,0:T(8,128)} %p_in.1, ...), custom_call_target="tpu_custom_call" | custom-call | tf_op jit(solution)/shard_map/pallas_call | solution.py:491
  56.5 0.0 copy-start.1
  56.5 1.6 %copy.22 = f32[3,8,8,128]{3,2,1,0:T(8,128)} copy(f32[3,8,8,128]{3,2,1,0:T(8,128)} %get-tuple-element.20) | data formatting | bytes 196608
  58.0 0.0 copy-done.1
  58.0 0.0 copy-start
  58.0 0.6 %copy.23 = f32[3,8,8,128]{3,2,1,0:T(8,128)} copy(f32[3,8,8,128]{3,2,1,0:T(8,128)S(1)} %copy-done.1) | data formatting | bytes 196608
  58.7 0.3 copy-done
  59.0 0.0 copy-start.2
  59.0 0.6 %copy.24 = f32[3,8,8,128]{3,2,1,0:T(8,128)} copy(f32[3,8,8,128]{3,2,1,0:T(8,128)S(1)} %copy-done) | data formatting | bytes 196608
  59.6 0.0 copy-done.2
  59.6 0.6 copy.25
Async XLA Ops:
  56.5 1.6 %copy-start.1 = (f32[3,8,8,128]{3,2,1,0:T(8,128)S(1)}, f32[3,8,8,128]{3,2,1,0:T(8,128)}, u32[]{:S(2)}) copy-start(f32[3,8,8,128]{3,2,1,0:T(8,128)} %get-tuple-element.21) | copy-start | bytes 294916
  58.0 0.9 %copy-start = (f32[3,8,8,128]{3,2,1,0:T(8,128)S(1)}, f32[3,8,8,128]{3,2,1,0:T(8,128)}, u32[]{:S(2)}) copy-start(f32[3,8,8,128]{3,2,1,0:T(8,128)} %get-tuple-element.22) | copy-start | bytes 294916
  59.0 0.7 %copy-start.2 = (f32[4,1,128]{2,1,0:T(1,128)S(1)}, f32[4,1,128]{2,1,0:T(1,128)}, u32[]{:S(2)}) copy-start(f32[4,1,128]{2,1,0:T(1,128)} %get-tuple-element.11) | copy-start | bytes 6148

commit v2 on v1

--- a/solution.py
+++ b/solution.py
@@ -40,6 +40,18 @@
     sine_out = jnp.where((quadrant & 2) != 0, -sine_part, sine_part)
     cosine_out = jnp.where(((quadrant + 1) & 2) != 0, -cosine_part, cosine_part)
     return cosine_out, sine_out
+
+
+def write_out(*refs):
+    sources, targets, sems = refs[0:4], refs[4:8], refs[8]
+    copies = [
+        pltpu.make_async_copy(source, target, sems.at[index])
+        for index, (source, target) in enumerate(zip(sources, targets))
+    ]
+    for copy in copies:
+        copy.start()
+    for copy in copies:
+        copy.wait()
 
 
 def make_kernel(sizes):
@@ -90,6 +102,7 @@
         ag_recv,
         gx_send,
         gx_recv,
+        row_sem,
     ):
         gx = lax.axis_index("gx")
         gy = lax.axis_index("gy")
@@ -112,13 +125,8 @@
             copy.start()
 
         barrier = pltpu.get_barrier_semaphore()
-        for place in ((left, above), (right, below)):
+        for place in ((left, gy), (right, gy), (left, above), (right, below)):
             pl.semaphore_signal(barrier, inc=1, device_id=place, device_id_type=MESH)
-
-        def greet_row(step, carry):
-            place = (lax.rem(gx + step, gx_count), gy)
-            pl.semaphore_signal(barrier, inc=1, device_id=place, device_id_type=MESH)
-            return carry
 
         def greet_column(step, carry):
             place = (gx, lax.rem(gy + step, gy_count))
@@ -126,49 +134,16 @@
             return carry
 
         lax.fori_loop(1, gy_count, greet_column, 0)
-        lax.fori_loop(1, gx_count, greet_row, 0)
-
-        omega = math.pi * (slot[...].astype(F32) + 0.5) / SPECTRUM_POINTS
-        uz_own = -0.7 + 1.4 * (jnp.full((1, freqs), uz_index[gy], jnp.int32).astype(F32) + 0.5) / AGRID
-        place_z = (lax.broadcasted_iota(jnp.int32, (depth, freqs), 0) - depth // 2).astype(F32)
-        cos_z, sin_z = sincos((omega * uz_own) * place_z)
-        TZ[:, 0:freqs] = cos_z
-        TZ[:, freqs:] = sin_z
-
-        sublane = lax.broadcasted_iota(jnp.int32, (8, freqs), 0)
-        ux_tiles = []
-        for tile in range(tiles):
-            labels = jnp.zeros((8, freqs), jnp.int32)
-            for row in range(8):
-                labels = jnp.where(sublane == row, ux_index[tile * 8 + row], labels)
-            ux_tiles.append(labels)
-        ux = -0.7 + 1.4 * (jnp.concatenate(ux_tiles, axis=0).astype(F32) + 0.5) / AGRID
-        omega_ux = omega * ux
-
-        def fill_x(cell, carry):
-            place_x = jnp.full((1, 1), gx * cx + cell - (gx_count * cx) // 2, jnp.int32).astype(F32)
-            cos_x, sin_x = sincos(omega_ux * place_x)
-            TX[0, cell] = cos_x
-            TX[1, cell] = sin_x
-            return carry
-
-        lax.fori_loop(0, cx, fill_x, 0)
-        uy = jnp.sqrt(1.0 - ux**2 - uz_own**2)
-        for face in range(2):
-            place_y = jnp.full((1, 1), box[2 + face] - (gy_count * cy) // 2, jnp.int32).astype(F32)
-            cos_y, sin_y = sincos((omega * uy) * place_y)
-            TY[face, 0] = cos_y
-            TY[face, 1] = sin_y
 
         for copy in local:
             copy.wait()
-        pl.semaphore_wait(barrier, gx_count - 1 + gy_count - 1 + 2)
+        pl.semaphore_wait(barrier, 4 + gy_count - 1)
 
         def halo(level):
             field = H.at[level]
             routes = [
                 (field.at[:, 0, 0:cy, :], field.at[:, cx, 0:cy, :], (left, gy)),
-                (field.at[:, cx - 1, 0:cy, :], field.at[:, cx + 1, 0:cy, :], (right, gy)),
+                (field.at[1:3, cx - 1, 0:cy, :], field.at[1:3, cx + 1, 0:cy, :], (right, gy)),
                 (field.at[:, 0:cx, 0, :], field.at[:, 0:cx, cy, :], (gx, below)),
                 (field.at[:, 0:cx, cy - 1, :], field.at[:, 0:cx, 2 * cy - 1, :], (gx, above)),
                 (field.at[0, 0, cy - 1, :], field.at[0, cx, 2 * cy - 1, :], (left, above)),
@@ -176,7 +151,7 @@
             ]
             if level == 0:
                 for ref in (E, J):
-                    routes.append((ref.at[:, 0, 0:cy, :], ref.at[:, cx, 0:cy, :], (left, gy)))
+                    routes.append((ref.at[1:3, 0, 0:cy, :], ref.at[1:3, cx, 0:cy, :], (left, gy)))
                     routes.append((ref.at[:, 0:cx, 0, :], ref.at[:, 0:cx, cy, :], (gx, below)))
                 for ref in (M, Q):
                     routes.append((ref.at[0, 0:cy, :], ref.at[cx, 0:cy, :], (left, gy)))
@@ -197,6 +172,38 @@
 
         pending = halo(0)
 
+        omega = math.pi * (slot[...].astype(F32) + 0.5) / SPECTRUM_POINTS
+        uz_own = -0.7 + 1.4 * (jnp.full((1, freqs), uz_index[gy], jnp.int32).astype(F32) + 0.5) / AGRID
+        place_z = (lax.broadcasted_iota(jnp.int32, (depth, freqs), 0) - depth // 2).astype(F32)
+        cos_z, sin_z = sincos((omega * uz_own) * place_z)
+        TZ[:, 0:freqs] = cos_z
+        TZ[:, freqs:] = sin_z
+
+        sublane = lax.broadcasted_iota(jnp.int32, (8, freqs), 0)
+        ux_tiles = []
+        for tile in range(tiles):
+            labels = jnp.zeros((8, freqs), jnp.int32)
+            for row in range(8):
+                labels = jnp.where(sublane == row, ux_index[tile * 8 + row], labels)
+            ux_tiles.append(labels)
+        ux = -0.7 + 1.4 * (jnp.concatenate(ux_tiles, axis=0).astype(F32) + 0.5) / AGRID
+        omega_ux = omega * ux
+
+        def fill_x(cell, carry):
+            place_x = jnp.full((1, 1), gx * cx + cell - (gx_count * cx) // 2, jnp.int32).astype(F32)
+            cos_x, sin_x = sincos(omega_ux * place_x)
+            TX[0, cell] = cos_x
+            TX[1, cell] = sin_x
+            return carry
+
+        lax.fori_loop(0, cx, fill_x, 0)
+        uy = jnp.sqrt(1.0 - ux**2 - uz_own**2)
+        for face in range(2):
+            place_y = jnp.full((1, 1), box[2 + face] - (gy_count * cy) // 2, jnp.int32).astype(F32)
+            cos_y, sin_y = sincos((omega * uy) * place_y)
+            TY[face, 0] = cos_y
+            TY[face, 1] = sin_y
+
         planes, rows = cx + 1, 2 * cy
         row = lax.broadcasted_iota(jnp.int32, (1, rows, depth), 1)
         lane = lax.broadcasted_iota(jnp.int32, (1, 1, depth), 2)
@@ -257,7 +264,7 @@
             total = jnp.sum(R[step], axis=1, keepdims=True)
             C[step, :, 0:1, :] = total
             copies = []
-            for offset in range(1, gy_count):
+            for offset in sorted(range(1, gy_count), key=lambda value: abs(value - gy_count // 2)):
                 other = lax.rem(gy + offset, gy_count)
                 copy = pltpu.make_async_remote_copy(
                     src_ref=C.at[step, :, pl.ds(0, 1), :],
@@ -271,6 +278,24 @@
                 copies.append(copy)
             G[step, :, pl.ds(gy, 1), :] = total
             return copies
+
+        greetings = []
+        known = 2
+        while known < gx_count // 2:
+            greetings.append(known)
+            known *= 2
+
+        def greet(level):
+            for shift in (greetings[level], gx_count - greetings[level]):
+                pl.semaphore_signal(
+                    row_sem.at[level],
+                    inc=1,
+                    device_id=(lax.rem(gx + shift, gx_count), gy),
+                    device_id_type=MESH,
+                )
+
+        def greeted(level):
+            pl.semaphore_wait(row_sem.at[level], 2)
 
         scatters = []
         gathers = []
@@ -305,6 +330,9 @@
                 K[1] = jnp.where(outside, 0.0, drive_e)
                 K[2] = keep_j
                 K[3] = drive_j
+            if step > 0:
+                greeted(step - 1)
+            greet(step)
             hx = H[step, 0, 0:planes]
             hy = H[step, 1, 0:planes]
             hz = H[step, 2, 0:planes]
@@ -337,7 +365,12 @@
             new_h = []
             for axis, turn in enumerate((first, second, third)):
                 value = H[step, axis, 0:cx, 0:cy] - DT * turn
-                H[step + 1, axis, 0:cx, 0:cy] = value
+                if step + 1 < STEPS:
+                    H[step + 1, axis, 0:cx, 0:cy] = value
+                else:
+                    h_out[axis] = value
+                    e_out[axis] = fresh[axis][0:cx, 0:cy]
+                    j_out[axis] = J[axis, 0:cx, 0:cy]
                 new_h.append(value)
             if step + 1 < STEPS:
                 pending = halo(step + 1)
@@ -348,13 +381,9 @@
                 for copy in scatters[step - 1]:
                     copy.wait_recv()
                 gathers.append(gather(step - 1))
-        results = [
-            pltpu.make_async_copy(E.at[:, 0:cx, 0:cy, :], e_out, local_sem.at[0]),
-            pltpu.make_async_copy(H.at[STEPS, :, 0:cx, 0:cy, :], h_out, local_sem.at[1]),
-            pltpu.make_async_copy(J.at[:, 0:cx, 0:cy, :], j_out, local_sem.at[2]),
-        ]
-        for copy in results:
-            copy.start()
+        for level in range(STEPS, len(greetings)):
+            greeted(level - 1)
+            greet(level)
         for copy in scatters[STEPS - 1]:
             copy.wait_recv()
         gathers.append(gather(STEPS - 1))
@@ -425,7 +454,9 @@
         TX[2, 1] = uy
         lax.fori_loop(0, tiles, project, 0)
 
-        def exchange(step):
+        def exchange(turn):
+            away = lax.div(turn, 2)
+            step = gx_count // 2 + jnp.where(lax.rem(turn, 2) == 0, away, -away)
             other = lax.rem(gx + step, gx_count)
             return pltpu.make_async_remote_copy(
                 src_ref=PART.at[:, pl.ds(other, 1), :],
@@ -436,25 +467,24 @@
                 device_id_type=MESH,
             )
 
-        def send(step, carry):
-            exchange(step).start()
+        def send(turn, carry):
+            exchange(turn).start()
             return carry
 
-        def receive(step, carry):
-            exchange(step).wait_recv()
+        def receive(turn, carry):
+            exchange(turn).wait_recv()
             return carry
 
-        def finish(step, carry):
-            exchange(step).wait_send()
+        def finish(turn, carry):
+            exchange(turn).wait_send()
             return carry
 
+        greeted(len(greetings) - 1)
         lax.fori_loop(1, gx_count, send, 0)
         RX[:, pl.ds(gx, 1), :] = PART[:, pl.ds(gx, 1), :]
         for group in halos, *scatters, *gathers:
             for copy in group:
                 copy.wait_send()
-        for copy in results:
-            copy.wait()
         lax.fori_loop(1, gx_count, receive, 0)
         far_out[...] = jnp.sum(RX[...], axis=1, keepdims=True)
         lax.fori_loop(1, gx_count, finish, 0)
@@ -487,15 +517,16 @@
         anywhere = pl.BlockSpec(memory_space=pl.ANY)
         scalars = pl.BlockSpec(memory_space=pltpu.SMEM)
         vectors = pl.BlockSpec(memory_space=pltpu.VMEM)
+        inner = pltpu.VMEM(e_field.shape, F32)
         field = jax.ShapeDtypeStruct(e_field.shape, F32)
         e_field, h_field, current, far = pl.pallas_call(
             make_kernel((gx_count, gy_count, cx, cy, depth, freqs, dirs_x)),
-            out_shape=(field, field, field, jax.ShapeDtypeStruct((4, 1, freqs), F32)),
+            out_shape=(inner, inner, inner, pltpu.VMEM((4, 1, freqs), F32)),
             in_specs=[anywhere] * 5 + [scalars] * 7 + [vectors],
-            out_specs=(anywhere, anywhere, anywhere, vectors),
+            out_specs=(vectors,) * 4,
             scratch_shapes=[
                 pltpu.VMEM((3, cx + 1, 2 * cy, depth), F32),
-                pltpu.VMEM((STEPS + 1, 3, cx + 2, 2 * cy, depth), F32),
+                pltpu.VMEM((STEPS, 3, cx + 2, 2 * cy, depth), F32),
                 pltpu.VMEM((3, cx + 1, 2 * cy, depth), F32),
                 pltpu.VMEM((cx + 1, 2 * cy, depth), jnp.int32),
                 pltpu.VMEM((cx + 1, 2 * cy, depth), jnp.int32),
@@ -519,6 +550,7 @@
                 pltpu.SemaphoreType.DMA((STEPS, gy_count)),
                 pltpu.SemaphoreType.DMA((gx_count,)),
                 pltpu.SemaphoreType.DMA((gx_count,)),
+                pltpu.SemaphoreType.REGULAR((8,)),
             ],
             compiler_params=pltpu.CompilerParams(collective_id=0, has_side_effects=True),
         )(
@@ -536,6 +568,18 @@
             uz_index,
             spectral_slot.reshape(1, freqs),
         )
+        e_field, h_field, current, far = pl.pallas_call(
+            write_out,
+            out_shape=(field, field, field, jax.ShapeDtypeStruct((4, 1, freqs), F32)),
+            in_specs=[vectors] * 4,
+            out_specs=(anywhere,) * 4,
+            scratch_shapes=[pltpu.SemaphoreType.DMA((4,))],
+        )(
+            *(
+                pltpu.with_memory_space_constraint(value, pltpu.VMEM)
+                for value in (e_field, h_field, current, far)
+            )
+        )
         return e_field, h_field, current, far.reshape(4, 1, 1, freqs)
 
     fields = P(None, "gx", "gy", None)

time: 60.4 us -> 54.5 us (0.902)
  local copies, waits for them, and re-layouts: 3.74 us -> 0 us
  Pallas kernels: 55.8 us -> 53.7 us
    unnamed x10 -> x0, local copies, waits for them, and re-layouts: 3.74 us -> none
    pallas_call x1, Pallas kernels: 55.8 us -> 53 us  [body(): pl.pallas_call(make_kernel((gx_count, gy_count, cx, cy, depth, freqs, dir...]
    pallas_call x0 -> x1, Pallas kernels: none -> 0.75 us  [body(): pl.pallas_call(write_out, out_shape=(field, field, field, jax.ShapeDtypeS...]
where the time goes in v2:
time: 54.5 us; the launch traced here: 54.4 us
  Pallas kernels  53.7 us (99%)
  between operations  0.64 us (1%)
    pallas_call x1, Pallas kernels, body(): pl.pallas_call(make_kernel((gx_count, gy_count, cx, cy, depth, freqs, dir...  53 us

profile of v2, /device:TPU:1, one launch (start us, length us, event | category | flops | bytes accessed | tf_op | source)
XLA Modules:
  0.0 54.4 jit_solution(15446629097664276221)
XLA Ops:
  0.6 53.0 %shard_map.156 = (f32[3,8,8,128]{3,2,1,0:T(8,128)S(1)}, f32[3,8,8,128]{3,2,1,0:T(8,128)S(1)}, f32[3,8,8,128]{3,2,1,0:T(8,128)S(1)}, f32[4,1,128]{2,1,0:T(1,128)S(1)}) custom-call(f32[3,8,8,128]{3,2,1,0:T(8,128)} %e_in.1, f32[3,8,8,128]{3,2,1,0:T(8,128)} %h_in.1, f32[3,8,8,128]{3,2,1,0:T(8,128)} %j_in.1, s32[8,8,128]{2,1,0:T(8,128)} %m_in.1, ...), custom_call_target="tpu_custom_call" | custom-call | tf_op jit(solution)/shard_map/pallas_call | solution.py:522
  53.6 0.7 %shard_map.157 = (f32[3,8,8,128]{3,2,1,0:T(8,128)}, f32[3,8,8,128]{3,2,1,0:T(8,128)}, f32[3,8,8,128]{3,2,1,0:T(8,128)}, f32[4,1,128]{2,1,0:T(1,128)}) custom-call(f32[3,8,8,128]{3,2,1,0:T(8,128)S(1)} %get-tuple-element.12.refs_0_, f32[3,8,8,128]{3,2,1,0:T(8,128)S(1)} %get-tuple-element.13.refs_1_, f32[3,8,8,128]{3,2,1,0:T(8,128)S(1)} %get-tuple-element.14.refs_2_, ...), custom_call_target="tpu_custom_call" | custom-call | tf_op jit(solution)/shard_map/pallas_call | solution.py:571

commit v3 on v2

--- a/solution.py
+++ b/solution.py
@@ -65,14 +65,14 @@
         j_in,
         m_in,
         p_in,
-        permittivity,
-        conductivity,
-        plasma,
-        damping,
-        box,
-        ux_index,
-        uz_index,
-        slot,
+        permittivity_in,
+        conductivity_in,
+        plasma_in,
+        damping_in,
+        box_in,
+        ux_in,
+        uz_in,
+        slot_in,
         e_out,
         h_out,
         j_out,
@@ -103,6 +103,14 @@
         gx_send,
         gx_recv,
         row_sem,
+        permittivity,
+        conductivity,
+        plasma,
+        damping,
+        box,
+        ux_index,
+        uz_index,
+        slot,
     ):
         gx = lax.axis_index("gx")
         gy = lax.axis_index("gy")
@@ -114,6 +122,17 @@
         member = lax.rem(gy, half)
 
         own = (slice(None), pl.ds(0, cx), pl.ds(0, cy))
+        barrier = pltpu.get_barrier_semaphore()
+        for place in ((left, gy), (right, gy), (left, above), (right, below)):
+            pl.semaphore_signal(barrier, inc=1, device_id=place, device_id_type=MESH)
+
+        def greet_column(step, carry):
+            place = (gx, lax.rem(gy + step, gy_count))
+            pl.semaphore_signal(barrier, inc=1, device_id=place, device_id_type=MESH)
+            return carry
+
+        lax.fori_loop(1, gy_count, greet_column, 0)
+
         local = [
             pltpu.make_async_copy(e_in, E.at[:, 0:cx, 0:cy, :], local_sem.at[0]),
             pltpu.make_async_copy(h_in, H.at[0, :, 0:cx, 0:cy, :], local_sem.at[1]),
@@ -121,41 +140,35 @@
             pltpu.make_async_copy(m_in, M.at[0:cx, 0:cy, :], local_sem.at[3]),
             pltpu.make_async_copy(p_in, Q.at[0:cx, 0:cy, :], local_sem.at[4]),
         ]
+        small = (permittivity_in, conductivity_in, plasma_in, damping_in, box_in, ux_in, uz_in)
+        held = (permittivity, conductivity, plasma, damping, box, ux_index, uz_index)
+        for index, (source, target) in enumerate(zip(small, held)):
+            local.append(pltpu.make_async_copy(source, target, local_sem.at[5 + index]))
+        local.append(pltpu.make_async_copy(slot_in, slot, local_sem.at[12]))
         for copy in local:
             copy.start()
 
-        barrier = pltpu.get_barrier_semaphore()
-        for place in ((left, gy), (right, gy), (left, above), (right, below)):
-            pl.semaphore_signal(barrier, inc=1, device_id=place, device_id_type=MESH)
-
-        def greet_column(step, carry):
-            place = (gx, lax.rem(gy + step, gy_count))
-            pl.semaphore_signal(barrier, inc=1, device_id=place, device_id_type=MESH)
-            return carry
-
-        lax.fori_loop(1, gy_count, greet_column, 0)
-
-        for copy in local:
-            copy.wait()
         pl.semaphore_wait(barrier, 4 + gy_count - 1)
 
         def halo(level):
             field = H.at[level]
+            held = h_in if level == 0 else field
+            last_x, last_y = cx - 1, cy - 1
             routes = [
-                (field.at[:, 0, 0:cy, :], field.at[:, cx, 0:cy, :], (left, gy)),
-                (field.at[1:3, cx - 1, 0:cy, :], field.at[1:3, cx + 1, 0:cy, :], (right, gy)),
-                (field.at[:, 0:cx, 0, :], field.at[:, 0:cx, cy, :], (gx, below)),
-                (field.at[:, 0:cx, cy - 1, :], field.at[:, 0:cx, 2 * cy - 1, :], (gx, above)),
-                (field.at[0, 0, cy - 1, :], field.at[0, cx, 2 * cy - 1, :], (left, above)),
-                (field.at[1, cx - 1, 0, :], field.at[1, cx + 1, cy, :], (right, below)),
+                (held.at[:, 0, 0:cy, :], field.at[:, cx, 0:cy, :], (left, gy)),
+                (held.at[1:3, last_x, 0:cy, :], field.at[1:3, cx + 1, 0:cy, :], (right, gy)),
+                (held.at[:, 0:cx, 0, :], field.at[:, 0:cx, cy, :], (gx, below)),
+                (held.at[:, 0:cx, last_y, :], field.at[:, 0:cx, 2 * cy - 1, :], (gx, above)),
+                (held.at[0, 0, last_y, :], field.at[0, cx, 2 * cy - 1, :], (left, above)),
+                (held.at[1, last_x, 0, :], field.at[1, cx + 1, cy, :], (right, below)),
             ]
             if level == 0:
-                for ref in (E, J):
-                    routes.append((ref.at[1:3, 0, 0:cy, :], ref.at[1:3, cx, 0:cy, :], (left, gy)))
-                    routes.append((ref.at[:, 0:cx, 0, :], ref.at[:, 0:cx, cy, :], (gx, below)))
-                for ref in (M, Q):
-                    routes.append((ref.at[0, 0:cy, :], ref.at[cx, 0:cy, :], (left, gy)))
-                    routes.append((ref.at[0:cx, 0, :], ref.at[0:cx, cy, :], (gx, below)))
+                for source, ref in ((e_in, E), (j_in, J)):
+                    routes.append((source.at[1:3, 0, :, :], ref.at[1:3, cx, 0:cy, :], (left, gy)))
+                    routes.append((source.at[:, :, 0, :], ref.at[:, 0:cx, cy, :], (gx, below)))
+                for source, ref in ((m_in, M), (p_in, Q)):
+                    routes.append((source.at[0, :, :], ref.at[cx, 0:cy, :], (left, gy)))
+                    routes.append((source.at[:, 0, :], ref.at[0:cx, cy, :], (gx, below)))
             copies = []
             for index, (source, target, place) in enumerate(routes):
                 copy = pltpu.make_async_remote_copy(
@@ -171,6 +184,8 @@
             return copies
 
         pending = halo(0)
+        for copy in local:
+            copy.wait()
 
         omega = math.pi * (slot[...].astype(F32) + 0.5) / SPECTRUM_POINTS
         uz_own = -0.7 + 1.4 * (jnp.full((1, freqs), uz_index[gy], jnp.int32).astype(F32) + 0.5) / AGRID
@@ -303,12 +318,7 @@
         for step in range(STEPS):
             for copy in pending:
                 copy.wait_recv()
-            if step == 0:
-                for copy in pending[6:10]:
-                    copy.wait_send()
-                halos.extend(pending[:6] + pending[10:])
-            else:
-                halos.extend(pending)
+            halos.extend(pending)
             if step == 0:
                 material = M[...]
                 pole = Q[...]
@@ -414,7 +424,7 @@
         uz_over = uz_own / sine_theta
         inverse = 1.0 / sine_theta
 
-        def project(tile, carry):
+        def project(tile):
             start = pl.multiple_of(tile * 8, 8)
             span = pl.ds(start, 8)
             sums = []
@@ -448,16 +458,12 @@
                 nx, nz, lx, lz = (turned[comp][part] for comp in range(4))
                 PART[part, span, :] = lx * ratio_b - nx * ratio_a + nz * sine_theta
                 PART[2 + part, span, :] = lx * ratio_a - lz * sine_theta + nx * ratio_b
-            return carry
 
         TX[2, 0] = ux + jnp.zeros((dirs_x, freqs), F32)
         TX[2, 1] = uy
-        lax.fori_loop(0, tiles, project, 0)
-
-        def exchange(turn):
-            away = lax.div(turn, 2)
-            step = gx_count // 2 + jnp.where(lax.rem(turn, 2) == 0, away, -away)
-            other = lax.rem(gx + step, gx_count)
+
+        def exchange(other):
+            step = lax.rem(other + gx_count - gx, gx_count)
             return pltpu.make_async_remote_copy(
                 src_ref=PART.at[:, pl.ds(other, 1), :],
                 dst_ref=RX.at[:, pl.ds(gx, 1), :],
@@ -467,20 +473,31 @@
                 device_id_type=MESH,
             )
 
-        def send(turn, carry):
-            exchange(turn).start()
+        def send(other, carry):
+            @pl.when(other != gx)
+            def _():
+                exchange(other).start()
+
             return carry
 
-        def receive(turn, carry):
-            exchange(turn).wait_recv()
+        def project_and_send(turn, carry):
+            away = lax.div(turn + 1, 2)
+            away = jnp.where(lax.rem(turn, 2) == 0, away, -away)
+            tile = lax.rem(lax.div(gx, 8) + tiles // 2 + away + tiles, tiles)
+            project(tile)
+            lax.fori_loop(tile * 8, tile * 8 + 8, send, 0)
             return carry
 
-        def finish(turn, carry):
-            exchange(turn).wait_send()
+        def receive(step, carry):
+            exchange(lax.rem(gx + step, gx_count)).wait_recv()
             return carry
 
+        def finish(step, carry):
+            exchange(lax.rem(gx + step, gx_count)).wait_send()
+            return carry
+
         greeted(len(greetings) - 1)
-        lax.fori_loop(1, gx_count, send, 0)
+        lax.fori_loop(0, tiles, project_and_send, 0)
         RX[:, pl.ds(gx, 1), :] = PART[:, pl.ds(gx, 1), :]
         for group in halos, *scatters, *gathers:
             for copy in group:
@@ -515,14 +532,13 @@
         freqs = spectral_slot.shape[0]
         dirs_x = ux_index.shape[0]
         anywhere = pl.BlockSpec(memory_space=pl.ANY)
-        scalars = pl.BlockSpec(memory_space=pltpu.SMEM)
         vectors = pl.BlockSpec(memory_space=pltpu.VMEM)
         inner = pltpu.VMEM(e_field.shape, F32)
         field = jax.ShapeDtypeStruct(e_field.shape, F32)
         e_field, h_field, current, far = pl.pallas_call(
             make_kernel((gx_count, gy_count, cx, cy, depth, freqs, dirs_x)),
             out_shape=(inner, inner, inner, pltpu.VMEM((4, 1, freqs), F32)),
-            in_specs=[anywhere] * 5 + [scalars] * 7 + [vectors],
+            in_specs=[anywhere] * 13,
             out_specs=(vectors,) * 4,
             scratch_shapes=[
                 pltpu.VMEM((3, cx + 1, 2 * cy, depth), F32),
@@ -541,7 +557,7 @@
                 pltpu.VMEM((2, 2, dirs_x, freqs), F32),
                 pltpu.VMEM((4, dirs_x, freqs), F32),
                 pltpu.VMEM((4, gx_count, freqs), F32),
-                pltpu.SemaphoreType.DMA((5,)),
+                pltpu.SemaphoreType.DMA((13,)),
                 pltpu.SemaphoreType.DMA((STEPS, 14)),
                 pltpu.SemaphoreType.DMA((STEPS, 14)),
                 pltpu.SemaphoreType.DMA((STEPS, cx)),
@@ -551,6 +567,14 @@
                 pltpu.SemaphoreType.DMA((gx_count,)),
                 pltpu.SemaphoreType.DMA((gx_count,)),
                 pltpu.SemaphoreType.REGULAR((8,)),
+                pltpu.SMEM(permittivity.shape, F32),
+                pltpu.SMEM(conductivity.shape, F32),
+                pltpu.SMEM(plasma.shape, F32),
+                pltpu.SMEM(damping.shape, F32),
+                pltpu.SMEM(box.shape, jnp.int32),
+                pltpu.SMEM(ux_index.shape, jnp.int32),
+                pltpu.SMEM(uz_index.shape, jnp.int32),
+                pltpu.VMEM((1, freqs), jnp.int32),
             ],
             compiler_params=pltpu.CompilerParams(collective_id=0, has_side_effects=True),
         )(

time: 54.5 us -> 55.1 us (1.011)
  Pallas kernels: 53.7 us -> 54.4 us
    pallas_call x1, Pallas kernels: 53 us -> 53.6 us  [body(): pl.pallas_call(make_kernel((gx_count, gy_count, cx, cy, depth, freqs, dir...]
where the time goes in v3:
time: 55.1 us; the launch traced here: 55 us
  Pallas kernels  54.4 us (99%)
  between operations  0.64 us (1%)
    pallas_call x1, Pallas kernels, body(): pl.pallas_call(make_kernel((gx_count, gy_count, cx, cy, depth, freqs, dir...  53.6 us

profile of v3, /device:TPU:1, one launch (start us, length us, event | category | flops | bytes accessed | tf_op | source)
XLA Modules:
  0.0 55.0 jit_solution(4465168539944125345)
XLA Ops:
  0.6 53.6 %shard_map.156 = (f32[3,8,8,128]{3,2,1,0:T(8,128)S(1)}, f32[3,8,8,128]{3,2,1,0:T(8,128)S(1)}, f32[3,8,8,128]{3,2,1,0:T(8,128)S(1)}, f32[4,1,128]{2,1,0:T(1,128)S(1)}) custom-call(f32[3,8,8,128]{3,2,1,0:T(8,128)} %e_in.1, f32[3,8,8,128]{3,2,1,0:T(8,128)} %h_in.1, f32[3,8,8,128]{3,2,1,0:T(8,128)} %j_in.1, s32[8,8,128]{2,1,0:T(8,128)} %m_in.1, ...), custom_call_target="tpu_custom_call" | custom-call | tf_op jit(solution)/shard_map/pallas_call | solution.py:538
  54.3 0.7 %shard_map.157 = (f32[3,8,8,128]{3,2,1,0:T(8,128)}, f32[3,8,8,128]{3,2,1,0:T(8,128)}, f32[3,8,8,128]{3,2,1,0:T(8,128)}, f32[4,1,128]{2,1,0:T(1,128)}) custom-call(f32[3,8,8,128]{3,2,1,0:T(8,128)S(1)} %get-tuple-element.12.refs_0_, f32[3,8,8,128]{3,2,1,0:T(8,128)S(1)} %get-tuple-element.13.refs_1_, f32[3,8,8,128]{3,2,1,0:T(8,128)S(1)} %get-tuple-element.14.refs_2_, ...), custom_call_target="tpu_custom_call" | custom-call | tf_op jit(solution)/shard_map/pallas_call | solution.py:595

commit v4 on v3

--- a/solution.py
+++ b/solution.py
@@ -10,6 +10,8 @@
 STEPS = 3
 SPECTRUM_POINTS = 512
 AGRID = 256
+LOW_FIRST, LOW_LAST = 1, 32
+HIGH_FIRST, HIGH_LAST = 96, 127
 DT = 0.5
 MESH = pl.DeviceIdType.MESH
 F32 = jnp.float32
@@ -56,7 +58,8 @@
 
 def make_kernel(sizes):
     gx_count, gy_count, cx, cy, depth, freqs, dirs_x = sizes
-    half = cx
+    owners = 4
+    share = cx // owners
     tiles = dirs_x // 8
 
     def kernel(
@@ -118,12 +121,10 @@
         right = lax.rem(gx + 1, gx_count)
         below = lax.rem(gy + gy_count - 1, gy_count)
         above = lax.rem(gy + 1, gy_count)
-        side = lax.div(gy, half)
-        member = lax.rem(gy, half)
 
         own = (slice(None), pl.ds(0, cx), pl.ds(0, cy))
         barrier = pltpu.get_barrier_semaphore()
-        for place in ((left, gy), (right, gy), (left, above), (right, below)):
+        for place in ((left, above), (right, below)):
             pl.semaphore_signal(barrier, inc=1, device_id=place, device_id_type=MESH)
 
         def greet_column(step, carry):
@@ -131,6 +132,18 @@
             pl.semaphore_signal(barrier, inc=1, device_id=place, device_id_type=MESH)
             return carry
 
+        def greet_row(shift, carry):
+            for place in (gx + shift, gx + gx_count - shift):
+                pl.semaphore_signal(
+                    barrier,
+                    inc=1,
+                    device_id=(lax.rem(place, gx_count), gy),
+                    device_id_type=MESH,
+                )
+            return carry
+
+        near = (gx_count // 2 + 1) // 2
+        lax.fori_loop(1, near + 1, greet_row, 0)
         lax.fori_loop(1, gy_count, greet_column, 0)
 
         local = [
@@ -148,7 +161,14 @@
         for copy in local:
             copy.start()
 
-        pl.semaphore_wait(barrier, 4 + gy_count - 1)
+        pl.semaphore_wait(barrier, 2 + 2 * near + gy_count - 1)
+        for place in (gx + near, gx + gx_count - near):
+            pl.semaphore_signal(
+                row_sem.at[0],
+                inc=1,
+                device_id=(lax.rem(place, gx_count), gy),
+                device_id_type=MESH,
+            )
 
         def halo(level):
             field = H.at[level]
@@ -258,62 +278,109 @@
         x_cell = lax.broadcasted_iota(jnp.int32, (cx, depth), 0) + gx * cx
         inside = jnp.where((x_cell >= box[0]) & (x_cell < box[1]), 1.0, 0.0)
 
+        low = gy < gy_count // 2
+        base = jnp.where(low, LOW_FIRST // cy, HIGH_FIRST // cy)
+        place = gy - base
+        members = jnp.where(low, LOW_LAST // cy, HIGH_LAST // cy) - base + 1
+        holds = (place >= 0) & (place < members)
+        collects = (place >= 0) & (place < owners)
+        quarter = jnp.where(low, 0, owners) + place
+        slots = 1 + max(LOW_LAST // cy - LOW_FIRST // cy, HIGH_LAST // cy - HIGH_FIRST // cy)
+
+        def to_owner(step, owner):
+            cells = pl.ds(owner * share, share)
+            return pltpu.make_async_remote_copy(
+                src_ref=S.at[step, :, cells, :],
+                dst_ref=R.at[step, place, :, cells, :],
+                send_sem=rs_send.at[step, owner],
+                recv_sem=rs_recv.at[step, place],
+                device_id=(gx, base + owner),
+                device_id_type=MESH,
+            )
+
+        def from_member(step, member):
+            cells = pl.ds(place * share, share)
+            return pltpu.make_async_remote_copy(
+                src_ref=S.at[step, :, cells, :],
+                dst_ref=R.at[step, member, :, cells, :],
+                send_sem=rs_send.at[step, 0],
+                recv_sem=rs_recv.at[step, member],
+                device_id=(gx, base + member),
+                device_id_type=MESH,
+            )
+
+        def to_column(step, offset):
+            return pltpu.make_async_remote_copy(
+                src_ref=C.at[step, :, pl.ds(place * share, share), :],
+                dst_ref=G.at[step, :, pl.ds(quarter * share, share), :],
+                send_sem=ag_send.at[step, offset],
+                recv_sem=ag_recv.at[step, quarter],
+                device_id=(gx, lax.rem(gy + offset, gy_count)),
+                device_id_type=MESH,
+            )
+
+        def from_column(step, part):
+            cells = pl.ds(part * share, share)
+            return pltpu.make_async_remote_copy(
+                src_ref=G.at[step, :, cells, :],
+                dst_ref=G.at[step, :, cells, :],
+                send_sem=ag_send.at[step, 0],
+                recv_sem=ag_recv.at[step, part],
+                device_id=(gx, above),
+                device_id_type=MESH,
+            )
+
         def scatter(step):
-            copies = []
-            for offset in range(1, half):
-                other = lax.rem(member + offset, half)
-                copy = pltpu.make_async_remote_copy(
-                    src_ref=S.at[step, :, pl.ds(other, 1), :],
-                    dst_ref=R.at[step, :, pl.ds(member, 1), :],
-                    send_sem=rs_send.at[step, offset],
-                    recv_sem=rs_recv.at[step, offset],
-                    device_id=(gx, side * half + other),
-                    device_id_type=MESH,
-                )
-                copy.start()
-                copies.append(copy)
-            R[step, :, pl.ds(member, 1), :] = S[step, :, pl.ds(member, 1), :]
-            return copies
+            for owner in range(owners):
+
+                @pl.when(holds & (place != owner))
+                def _():
+                    to_owner(step, owner).start()
+
+            @pl.when(collects)
+            def _():
+                R[step, place] = S[step]
 
         def gather(step):
-            total = jnp.sum(R[step], axis=1, keepdims=True)
-            C[step, :, 0:1, :] = total
-            copies = []
-            for offset in sorted(range(1, gy_count), key=lambda value: abs(value - gy_count // 2)):
-                other = lax.rem(gy + offset, gy_count)
-                copy = pltpu.make_async_remote_copy(
-                    src_ref=C.at[step, :, pl.ds(0, 1), :],
-                    dst_ref=G.at[step, :, pl.ds(gy, 1), :],
-                    send_sem=ag_send.at[step, offset],
-                    recv_sem=ag_recv.at[step, offset],
-                    device_id=(gx, other),
-                    device_id_type=MESH,
-                )
-                copy.start()
-                copies.append(copy)
-            G[step, :, pl.ds(gy, 1), :] = total
-            return copies
-
-        greetings = []
-        known = 2
-        while known < gx_count // 2:
-            greetings.append(known)
-            known *= 2
-
-        def greet(level):
-            for shift in (greetings[level], gx_count - greetings[level]):
-                pl.semaphore_signal(
-                    row_sem.at[level],
-                    inc=1,
-                    device_id=(lax.rem(gx + shift, gx_count), gy),
-                    device_id_type=MESH,
-                )
-
-        def greeted(level):
-            pl.semaphore_wait(row_sem.at[level], 2)
-
-        scatters = []
-        gathers = []
+            @pl.when(collects)
+            def _():
+                for member in range(slots):
+
+                    @pl.when((place != member) & (member < members))
+                    def _():
+                        from_member(step, member).wait_recv()
+
+                total = R[step, 0]
+                for member in range(1, slots):
+                    total = total + jnp.where(member < members, R[step, member], 0.0)
+                C[step] = total
+                for offset in sorted(range(1, gy_count), key=lambda value: abs(value - gy_count // 2)):
+                    to_column(step, offset).start()
+                for cell in range(share):
+                    G[step, :, pl.ds(quarter * share + cell, 1), :] = C[
+                        step, :, pl.ds(place * share + cell, 1), :
+                    ]
+
+        def gathered(step):
+            for part in range(2 * owners):
+                owner = part if part < owners else HIGH_FIRST // cy + part - owners
+
+                @pl.when(gy != owner)
+                def _():
+                    from_column(step, part).wait_recv()
+
+        def collected(step):
+            for owner in range(owners):
+
+                @pl.when(holds & (place != owner))
+                def _():
+                    to_owner(step, owner).wait_send()
+
+            @pl.when(collects)
+            def _():
+                for offset in range(1, gy_count):
+                    to_column(step, offset).wait_send()
+
         halos = []
         for step in range(STEPS):
             for copy in pending:
@@ -340,9 +407,6 @@
                 K[1] = jnp.where(outside, 0.0, drive_e)
                 K[2] = keep_j
                 K[3] = drive_j
-            if step > 0:
-                greeted(step - 1)
-            greet(step)
             hx = H[step, 0, 0:planes]
             hy = H[step, 1, 0:planes]
             hz = H[step, 2, 0:planes]
@@ -386,23 +450,15 @@
                 pending = halo(step + 1)
             for index, value in enumerate((new_h[2], -new_h[0], -ez_o, ex_o)):
                 S[step, index] = jnp.sum(value * face_weight, axis=1) * inside
-            scatters.append(scatter(step))
+            scatter(step)
             if step > 0:
-                for copy in scatters[step - 1]:
-                    copy.wait_recv()
-                gathers.append(gather(step - 1))
-        for level in range(STEPS, len(greetings)):
-            greeted(level - 1)
-            greet(level)
-        for copy in scatters[STEPS - 1]:
-            copy.wait_recv()
-        gathers.append(gather(STEPS - 1))
+                gather(step - 1)
+        gather(STEPS - 1)
 
         real = [jnp.zeros((8, freqs), F32) for _ in range(8)]
         imag = [jnp.zeros((8, freqs), F32) for _ in range(8)]
         for step in range(STEPS):
-            for copy in gathers[step]:
-                copy.wait_recv()
+            gathered(step)
             lines = jnp.dot(
                 G[step].reshape(4 * gy_count, depth),
                 TZ[...],
@@ -496,12 +552,13 @@
             exchange(lax.rem(gx + step, gx_count)).wait_send()
             return carry
 
-        greeted(len(greetings) - 1)
+        pl.semaphore_wait(row_sem.at[0], 2)
         lax.fori_loop(0, tiles, project_and_send, 0)
         RX[:, pl.ds(gx, 1), :] = PART[:, pl.ds(gx, 1), :]
-        for group in halos, *scatters, *gathers:
-            for copy in group:
-                copy.wait_send()
+        for copy in halos:
+            copy.wait_send()
+        for step in range(STEPS):
+            collected(step)
         lax.fori_loop(1, gx_count, receive, 0)
         far_out[...] = jnp.sum(RX[...], axis=1, keepdims=True)
         lax.fori_loop(1, gx_count, finish, 0)
@@ -548,7 +605,7 @@
                 pltpu.VMEM((cx + 1, 2 * cy, depth), jnp.int32),
                 pltpu.VMEM((4, cx + 1, 2 * cy, depth), F32),
                 pltpu.VMEM((STEPS, 4, cx, depth), F32),
-                pltpu.VMEM((STEPS, 4, cx, depth), F32),
+                pltpu.VMEM((STEPS, 5, 4, cx, depth), F32),
                 pltpu.VMEM((STEPS, 4, 8, depth), F32),
                 pltpu.VMEM((STEPS, 4, gy_count, depth), F32),
                 pltpu.VMEM((8, 2, cx, freqs), F32),
@@ -566,7 +623,7 @@
                 pltpu.SemaphoreType.DMA((STEPS, gy_count)),
                 pltpu.SemaphoreType.DMA((gx_count,)),
                 pltpu.SemaphoreType.DMA((gx_count,)),
-                pltpu.SemaphoreType.REGULAR((8,)),
+                pltpu.SemaphoreType.REGULAR((1,)),
                 pltpu.SMEM(permittivity.shape, F32),
                 pltpu.SMEM(conductivity.shape, F32),
                 pltpu.SMEM(plasma.shape, F32),

time: 55.1 us -> 53.8 us (0.976)
  Pallas kernels: 54.4 us -> 53 us
    pallas_call x1, Pallas kernels: 53.6 us -> 52.3 us  [body(): pl.pallas_call(make_kernel((gx_count, gy_count, cx, cy, depth, freqs, dir...]
where the time goes in v4:
time: 53.8 us; the launch traced here: 53.7 us
  Pallas kernels  53 us (99%)
  between operations  0.64 us (1%)
    pallas_call x1, Pallas kernels, body(): pl.pallas_call(make_kernel((gx_count, gy_count, cx, cy, depth, freqs, dir...  52.3 us

profile of v4, /device:TPU:1, one launch (start us, length us, event | category | flops | bytes accessed | tf_op | source)
XLA Modules:
  0.0 53.7 jit_solution(8537532464650762317)
XLA Ops:
  0.6 52.3 %shard_map.156 = (f32[3,8,8,128]{3,2,1,0:T(8,128)S(1)}, f32[3,8,8,128]{3,2,1,0:T(8,128)S(1)}, f32[3,8,8,128]{3,2,1,0:T(8,128)S(1)}, f32[4,1,128]{2,1,0:T(1,128)S(1)}) custom-call(f32[3,8,8,128]{3,2,1,0:T(8,128)} %e_in.1, f32[3,8,8,128]{3,2,1,0:T(8,128)} %h_in.1, f32[3,8,8,128]{3,2,1,0:T(8,128)} %j_in.1, s32[8,8,128]{2,1,0:T(8,128)} %m_in.1, ...), custom_call_target="tpu_custom_call" | custom-call | tf_op jit(solution)/shard_map/pallas_call | solution.py:595
  52.9 0.7 %shard_map.157 = (f32[3,8,8,128]{3,2,1,0:T(8,128)}, f32[3,8,8,128]{3,2,1,0:T(8,128)}, f32[3,8,8,128]{3,2,1,0:T(8,128)}, f32[4,1,128]{2,1,0:T(1,128)}) custom-call(f32[3,8,8,128]{3,2,1,0:T(8,128)S(1)} %get-tuple-element.12.refs_0_, f32[3,8,8,128]{3,2,1,0:T(8,128)S(1)} %get-tuple-element.13.refs_1_, f32[3,8,8,128]{3,2,1,0:T(8,128)S(1)} %get-tuple-element.14.refs_2_, ...), custom_call_target="tpu_custom_call" | custom-call | tf_op jit(solution)/shard_map/pallas_call | solution.py:652

commit v5 on v4

--- a/solution.py
+++ b/solution.py
@@ -124,15 +124,17 @@
 
         own = (slice(None), pl.ds(0, cx), pl.ds(0, cy))
         barrier = pltpu.get_barrier_semaphore()
-        for place in ((left, above), (right, below)):
-            pl.semaphore_signal(barrier, inc=1, device_id=place, device_id_type=MESH)
-
-        def greet_column(step, carry):
-            place = (gx, lax.rem(gy + step, gy_count))
+        def middle_out(turn):
+            away = lax.div(turn + 1, 2)
+            return gy_count // 2 + jnp.where(lax.rem(turn, 2) == 0, away, -away)
+
+        def greet_column(turn, carry):
+            place = (gx, lax.rem(gy + middle_out(turn), gy_count))
             pl.semaphore_signal(barrier, inc=1, device_id=place, device_id_type=MESH)
             return carry
 
-        def greet_row(shift, carry):
+        def greet_row(turn, carry):
+            shift = near - turn
             for place in (gx + shift, gx + gx_count - shift):
                 pl.semaphore_signal(
                     barrier,
@@ -143,8 +145,10 @@
             return carry
 
         near = (gx_count // 2 + 1) // 2
-        lax.fori_loop(1, near + 1, greet_row, 0)
-        lax.fori_loop(1, gy_count, greet_column, 0)
+        lax.fori_loop(0, near, greet_row, 0)
+        lax.fori_loop(0, gy_count - 1, greet_column, 0)
+        for place in ((left, above), (right, below)):
+            pl.semaphore_signal(barrier, inc=1, device_id=place, device_id_type=MESH)
 
         local = [
             pltpu.make_async_copy(e_in, E.at[:, 0:cx, 0:cy, :], local_sem.at[0]),
@@ -354,8 +358,12 @@
                 for member in range(1, slots):
                     total = total + jnp.where(member < members, R[step, member], 0.0)
                 C[step] = total
-                for offset in sorted(range(1, gy_count), key=lambda value: abs(value - gy_count // 2)):
-                    to_column(step, offset).start()
+
+                def send_column(turn, carry):
+                    to_column(step, middle_out(turn)).start()
+                    return carry
+
+                lax.fori_loop(0, gy_count - 1, send_column, 0)
                 for cell in range(share):
                     G[step, :, pl.ds(quarter * share + cell, 1), :] = C[
                         step, :, pl.ds(place * share + cell, 1), :
@@ -378,8 +386,12 @@
 
             @pl.when(collects)
             def _():
-                for offset in range(1, gy_count):
+
+                def sent_column(offset, carry):
                     to_column(step, offset).wait_send()
+                    return carry
+
+                lax.fori_loop(1, gy_count, sent_column, 0)
 
         halos = []
         for step in range(STEPS):
@@ -441,10 +453,6 @@
                 value = H[step, axis, 0:cx, 0:cy] - DT * turn
                 if step + 1 < STEPS:
                     H[step + 1, axis, 0:cx, 0:cy] = value
-                else:
-                    h_out[axis] = value
-                    e_out[axis] = fresh[axis][0:cx, 0:cy]
-                    j_out[axis] = J[axis, 0:cx, 0:cy]
                 new_h.append(value)
             if step + 1 < STEPS:
                 pending = halo(step + 1)
@@ -453,6 +461,10 @@
             scatter(step)
             if step > 0:
                 gather(step - 1)
+        for axis in range(3):
+            h_out[axis] = new_h[axis]
+            e_out[axis] = E[axis, 0:cx, 0:cy]
+            j_out[axis] = J[axis, 0:cx, 0:cy]
         gather(STEPS - 1)
 
         real = [jnp.zeros((8, freqs), F32) for _ in range(8)]

time: 53.8 us -> 54.2 us (level)
  no operation moved by 1% of the time
where the time goes in v5:
time: 54.2 us; the launch traced here: 54 us
  Pallas kernels  53.4 us (99%)
  between operations  0.64 us (1%)
    pallas_call x1, Pallas kernels, body(): pl.pallas_call(make_kernel((gx_count, gy_count, cx, cy, depth, freqs, dir...  52.7 us

profile of v5, /device:TPU:1, one launch (start us, length us, event | category | flops | bytes accessed | tf_op | source)
XLA Modules:
  0.0 54.0 jit_solution(63594907990557672)
XLA Ops:
  0.6 52.7 %shard_map.156 = (f32[3,8,8,128]{3,2,1,0:T(8,128)S(1)}, f32[3,8,8,128]{3,2,1,0:T(8,128)S(1)}, f32[3,8,8,128]{3,2,1,0:T(8,128)S(1)}, f32[4,1,128]{2,1,0:T(1,128)S(1)}) custom-call(f32[3,8,8,128]{3,2,1,0:T(8,128)} %e_in.1, f32[3,8,8,128]{3,2,1,0:T(8,128)} %h_in.1, f32[3,8,8,128]{3,2,1,0:T(8,128)} %j_in.1, s32[8,8,128]{2,1,0:T(8,128)} %m_in.1, ...), custom_call_target="tpu_custom_call" | custom-call | tf_op jit(solution)/shard_map/pallas_call | solution.py:607
  53.3 0.7 %shard_map.157 = (f32[3,8,8,128]{3,2,1,0:T(8,128)}, f32[3,8,8,128]{3,2,1,0:T(8,128)}, f32[3,8,8,128]{3,2,1,0:T(8,128)}, f32[4,1,128]{2,1,0:T(1,128)}) custom-call(f32[3,8,8,128]{3,2,1,0:T(8,128)S(1)} %get-tuple-element.12.refs_0_, f32[3,8,8,128]{3,2,1,0:T(8,128)S(1)} %get-tuple-element.13.refs_1_, f32[3,8,8,128]{3,2,1,0:T(8,128)S(1)} %get-tuple-element.14.refs_2_, ...), custom_call_target="tpu_custom_call" | custom-call | tf_op jit(solution)/shard_map/pallas_call | solution.py:664
